TPU v7x, 32 devices: a whole 2x2x4 slice. The times are simulated.
32 devices in a mesh: groups: 2 (over y), seq: 4 (over z), rep: 4 (over x, core).
Axes of the slice: x: 2, y: 2, z: 4, core: 2. Of those that a mesh axis runs over, the one named last changes fastest.
Arguments:
- points: bfloat16 [65536, 256], P(('groups', 'seq', 'rep')), parts along dimension 0, may hold values from -8 to 8
- ball_order: int32 [32, 2048], P(('groups', 'seq', 'rep')), parts along dimension 0, may hold values from 0 to 2047, as said below
- ball_counts: int32 [512], P(('groups', 'seq', 'rep')), parts along dimension 0, may hold values from 1 to 128
- gain_attn: float32 [256], replicated, may hold values from 0.25 to 1.75
- gain_mlp: float32 [256], replicated, may hold values from 0.25 to 1.75
- head_temps: float32 [2, 8], replicated, may hold values from 2 to 6
- w_qkv: bfloat16 [256, 768], replicated, may hold values from -0.375 to 0.375
- w_out: bfloat16 [256, 256], replicated, may hold values from -0.375 to 0.375
- c_qkv: bfloat16 [256, 768], replicated, may hold values from -0.375 to 0.375
- c_out: bfloat16 [256, 256], replicated, may hold values from -0.375 to 0.375
- w_up: bfloat16 [256, 1024], replicated, may hold values from -0.375 to 0.375
- w_down: bfloat16 [1024, 256], replicated, may hold values from -0.1875 to 0.1875
Outputs:
- layer_out: bfloat16 [65536, 256], P(('groups', 'seq', 'rep')), parts along dimension 0
There are 2 independent parts, one for each index of `groups`. A program takes and returns all parts, laid end to end along the dimension named above; an argument that names none is the same for every part. Nothing has to cross between parts.
Inputs may be any that keep to these rules, and one draw needn't show every extreme that they name: `ball_order`: each row is a permutation of 0 to 2047: for every ball-ordered position of a device's block, the row of that block in stored order. `ball_counts`: valid points of each ball of 128 consecutive ball-ordered rows; the valid ones come first.
All inputs are finite; a program needn't handle non-finite values.
Results may differ from a plain program's by a relative error of at most 0.009.
Values may be sent and summed in bfloat16 or wider, within the bound.
A program may use at most 128 MiB of HBM per device.

v0:
```python
import functools
import math

import jax
import jax.numpy as jnp
from jax import lax
from jax.experimental import pallas as pl
from jax.experimental.pallas import tpu as pltpu
from jax.sharding import PartitionSpec as P

BALL = 128
POOL = 64
EPS = 1e-06
VMEM_ATTEND = 61 << 20
VMEM_MLP = 61 << 20
LANES = 128
GELU_A = math.sqrt(2.0 / math.pi)
GELU_B = 0.044715 * math.sqrt(2.0 / math.pi)
LOG2E = 1.4426950408889634
MESH = pl.DeviceIdType.MESH
BF = jnp.bfloat16
F32 = jnp.float32


def dot(a, b):
    return jnp.dot(a, b, preferred_element_type=F32)


def dot_t(a, b):
    return lax.dot_general(a, b, (((1,), (1,)), ((), ())), preferred_element_type=F32)


def gelu(upward):
    inner = upward * (GELU_A + GELU_B * (upward * upward))
    return (0.5 * upward * (1.0 + jnp.tanh(inner))).astype(BF)


def rms(values, gain):
    return values * lax.rsqrt(jnp.mean(values * values, axis=-1, keepdims=True) + EPS) * gain


def attend_kernel(
    sizes,
    points,
    order,
    counts,
    gain_attn,
    temps,
    w_qkv_hbm,
    w_out_hbm,
    c_qkv_hbm,
    c_out_hbm,
    mid_out,
    coarse,
    srt,
    nrm,
    mid,
    stage,
    tokens_all,
    w_qkv,
    w_out,
    c_qkv,
    c_out,
    load_sem,
    out_sem,
    local_sem,
    seq_send,
    rep_send,
    recv_sem,
):
    seq_n, rep_n, heads = sizes
    peers = seq_n * rep_n
    rows, width = points.shape
    head_dim = width // heads
    chunk = 4 * BALL
    chunks = rows // chunk
    tokens = chunk // POOL
    coarse_rows = rows // POOL
    my_seq = lax.axis_index("seq")
    my_rep = lax.axis_index("rep")
    me = my_seq * rep_n + my_rep

    loads = [
        pltpu.make_async_copy(source, target, load_sem.at[n])
        for n, (source, target) in enumerate(
            [(w_qkv_hbm, w_qkv), (w_out_hbm, w_out), (c_qkv_hbm, c_qkv), (c_out_hbm, c_out)]
        )
    ]
    for load in loads:
        load.start()

    barrier = pltpu.get_barrier_semaphore()

    def greet_seq(step, carry):
        place = {"seq": lax.rem(my_seq + step, seq_n), "rep": my_rep}
        pl.semaphore_signal(barrier, inc=1, device_id=place, device_id_type=MESH)
        return carry

    def greet_rep(step, carry):
        place = {"seq": my_seq, "rep": lax.rem(my_rep + step, rep_n)}
        pl.semaphore_signal(barrier, inc=1, device_id=place, device_id_type=MESH)
        return carry

    lax.fori_loop(1, seq_n, greet_seq, 0)
    lax.fori_loop(1, rep_n, greet_rep, 0)

    lane_head = lax.broadcasted_iota(jnp.int32, (1, width), 1) // head_dim
    near_heads = LANES // head_dim
    slabs = [slice(g * LANES, (g + 1) * LANES) for g in range(width // LANES)]
    near = lax.broadcasted_iota(jnp.int32, (1, LANES), 1) // head_dim
    head_lanes = [(near == h).astype(F32).astype(BF) for h in range(near_heads)]

    def by_head(block):
        return jnp.concatenate([block * lanes for lanes in head_lanes], axis=0)

    block_mean = jnp.where(
        lax.broadcasted_iota(jnp.int32, (width, width), 0) // head_dim
        == lax.broadcasted_iota(jnp.int32, (width, width), 1) // head_dim,
        1.0 / head_dim,
        0.0,
    ).astype(BF)

    def lane_scale(row):
        scale = jnp.zeros((1, width), F32)
        for h in range(heads):
            scale = jnp.where(lane_head == h, temps[row, h], scale)
        return scale * (LOG2E / math.sqrt(head_dim))

    def head_rms(values):
        return values * lax.rsqrt(dot((values * values).astype(BF), block_mean) + EPS)

    gain_a = gain_attn[...]

    def gather_chunk(i, carry):
        base = pl.multiple_of(i * chunk, chunk)
        picks = []
        lane = lax.broadcasted_iota(jnp.int32, (BALL, BALL), 1).astype(F32)
        for b in range(4):
            row = order[:, pl.ds(base + b * BALL, BALL)].astype(F32)
            column = jnp.transpose(jnp.broadcast_to(row, (BALL, BALL)))
            picks.append(
                jnp.concatenate(
                    [
                        jnp.where(column == lane + float(j * BALL), 1.0, 0.0).astype(BF)
                        for j in range(rows // BALL)
                    ],
                    axis=1,
                )
            )
        sorted_rows = dot(jnp.concatenate(picks, axis=0), points[...])
        srt[pl.ds(base, chunk), :] = sorted_rows.astype(BF)
        normed = rms(sorted_rows, gain_a).astype(BF)
        nrm[pl.ds(base, chunk), :] = normed
        shape = (2 * tokens, chunk)
        token = lax.broadcasted_iota(jnp.int32, shape, 0)
        place = lax.broadcasted_iota(jnp.int32, shape, 1)
        half = jnp.zeros(shape, jnp.int32)
        for b in range(4):
            half = jnp.where(token // 2 == b, counts[i * 4 + b], half)
        half = jnp.clip(half - POOL * (token % 2), 0, POOL)
        offset = place - token * POOL
        take = jnp.where((offset >= 0) & (offset < half), 1.0, 0.0).astype(BF)
        total = dot(take, normed)[:tokens]
        half_f = half[:tokens, :width].astype(F32)
        spot = pl.ds(pl.multiple_of(i * tokens, tokens), tokens)
        stage[spot, :width] = total / jnp.maximum(half_f, 1.0)
        stage[spot, width:] = jnp.where(half_f[:, :128] > 0.0, 1.0, 0.0)
        return carry

    lax.fori_loop(0, chunks, gather_chunk, 0)

    own_block = stage[...].astype(BF)
    tokens_all[me] = own_block

    pl.semaphore_wait(barrier, seq_n + rep_n - 2)

    def seq_copy(step):
        return pltpu.make_async_remote_copy(
            src_ref=tokens_all.at[me],
            dst_ref=tokens_all.at[me],
            send_sem=seq_send.at[step],
            recv_sem=recv_sem.at[me],
            device_id={"seq": lax.rem(my_seq + step, seq_n), "rep": my_rep},
            device_id_type=MESH,
        )

    def rep_copy(away, step):
        block = lax.rem(my_seq + away, seq_n) * rep_n + my_rep
        return pltpu.make_async_remote_copy(
            src_ref=tokens_all.at[block],
            dst_ref=tokens_all.at[block],
            send_sem=rep_send.at[away, step],
            recv_sem=recv_sem.at[block],
            device_id={"seq": my_seq, "rep": lax.rem(my_rep + step, rep_n)},
            device_id_type=MESH,
        )

    def arrival(block):
        return pltpu.make_async_remote_copy(
            src_ref=tokens_all.at[block],
            dst_ref=tokens_all.at[block],
            send_sem=seq_send.at[0],
            recv_sem=recv_sem.at[block],
            device_id={"seq": lax.rem(my_seq + 1, seq_n), "rep": my_rep},
            device_id_type=MESH,
        )

    def each(count, first, act):
        def body(step, carry):
            act(step)
            return carry

        lax.fori_loop(first, count, body, 0)

    each(seq_n, 1, lambda step: seq_copy(step).start())
    each(rep_n, 1, lambda step: rep_copy(0, step).start())

    def relay(away):
        arrival(lax.rem(my_seq + away, seq_n) * rep_n + my_rep).wait_recv()
        each(rep_n, 1, lambda step: rep_copy(away, step).start())

    for load in loads:
        load.wait()

    q_scale = lane_scale(0)

    def ball_chunk(i, carry):
        base = pl.multiple_of(i * chunk, chunk)
        spot = pl.ds(base, chunk)
        joined = dot(nrm[spot, :], w_qkv[...])
        q = (head_rms(joined[:, :width]) * q_scale).astype(BF)
        k = head_rms(joined[:, width : 2 * width]).astype(BF)
        v = joined[:, 2 * width :]
        mixes = []
        for b in range(4):
            part = slice(b * BALL, (b + 1) * BALL)
            live = lax.broadcasted_iota(jnp.int32, (BALL, width), 0) < counts[i * 4 + b]
            vb = jnp.where(live, v[part], 0.0).astype(BF)
            ones = by_head(jnp.where(live[:, :LANES], 1.0, 0.0).astype(BF))
            slab_mixes = []
            for slab in slabs:
                weights = jnp.exp2(dot_t(q[part, slab], by_head(k[part, slab]))).astype(BF)
                mixed = dot(weights, jnp.concatenate([by_head(vb[:, slab]), ones], axis=1))
                slab_mixes.append((mixed[:, :LANES] / mixed[:, LANES:]).astype(BF))
            mixes.append(jnp.concatenate(slab_mixes, axis=1))
        fine = dot(jnp.concatenate(mixes, axis=0), w_out[...])
        mid[spot, :] = (srt[spot, :].astype(F32) + fine).astype(BF)
        return carry

    def leave(i):
        spot = pl.ds(pl.multiple_of(i * chunk, chunk), chunk)
        return pltpu.make_async_copy(mid.at[spot, :], mid_out.at[spot, :], out_sem.at[i])

    def ball_step(i, carry):
        ball_chunk(i, carry)
        leave(i).start()
        return carry

    early = chunks // 2
    lax.fori_loop(0, early, ball_step, 0)
    each(seq_n, 1, relay)
    lax.fori_loop(early, chunks, ball_step, 0)

    q_c = dot(own_block[:, :width], c_qkv[:, :width])
    q_c = (head_rms(q_c) * lane_scale(1)).astype(BF)
    queries = [by_head(q_c[:, slab]) for slab in slabs]

    def gathered(step):
        def one(away):
            rep = lax.rem(my_rep + step, rep_n)
            arrival(lax.rem(my_seq + away, seq_n) * rep_n + rep).wait_recv()

        each(seq_n, 0, one)

    each(rep_n, 1, gathered)

    group = math.gcd(peers, 16)

    def coarse_keys(g):
        block = tokens_all[pl.ds(g * group, group)].reshape(group * coarse_rows, width + 128)
        joined = dot(block[:, :width], c_qkv[:, width:])
        keys = head_rms(joined[:, :width]).astype(BF)
        values = joined[:, width:].astype(BF)
        sums = []
        for query, slab in zip(queries, slabs):
            weights = jnp.exp2(dot_t(query, keys[:, slab])).astype(BF)
            sums.append(dot(weights, jnp.concatenate([values[:, slab], block[:, width:]], axis=1)))
        return sums

    if peers == group:
        sums = coarse_keys(0)
    else:
        sums = lax.fori_loop(
            0,
            peers // group,
            lambda g, total: [a + b for a, b in zip(total, coarse_keys(g))],
            [jnp.zeros((near_heads * coarse_rows, 2 * LANES), F32) for _ in slabs],
        )
    slab_mixes = []
    for total in sums:
        ratio = total[:, :LANES] / total[:, LANES:]
        mix = jnp.zeros((coarse_rows, LANES), F32)
        for h in range(near_heads):
            mix = jnp.where(near == h, ratio[h * coarse_rows : (h + 1) * coarse_rows], mix)
        slab_mixes.append(mix)
    mix = jnp.concatenate(slab_mixes, axis=1)
    coarse[...] = dot(mix.astype(BF), c_out[...])

    each(seq_n, 1, lambda step: seq_copy(step).wait_send())
    each(seq_n, 0, lambda away: each(rep_n, 1, lambda step: rep_copy(away, step).wait_send()))
    each(chunks, 0, lambda i: leave(i).wait())


def mlp_kernel(
    mid_hbm,
    coarse,
    order,
    gain_mlp,
    w_up_hbm,
    w_down_hbm,
    out,
    mid,
    w_up,
    w_down,
    res,
    ready,
    mid_sem,
    load_sem,
    out_sem,
):
    rows, width = mid.shape
    chunk = 4 * BALL
    chunks = rows // chunk
    tokens = chunk // POOL
    gain_m = gain_mlp[...]

    def enter(i):
        spot = pl.ds(pl.multiple_of(i * chunk, chunk), chunk)
        return pltpu.make_async_copy(mid_hbm.at[spot, :], mid.at[spot, :], mid_sem.at[i])

    load_up = pltpu.make_async_copy(w_up_hbm, w_up, load_sem.at[0])
    load_down = pltpu.make_async_copy(w_down_hbm, w_down, load_sem.at[1])
    enter(0).start()
    load_up.start()
    load_down.start()
    for i in range(1, chunks):
        enter(i).start()
    load_up.wait()
    load_down.wait()

    def mlp_chunk(i, carry):
        enter(i).wait()
        spot = pl.ds(pl.multiple_of(i * chunk, chunk), chunk)
        terms = coarse[pl.ds(pl.multiple_of(i * tokens, tokens), tokens), :]
        spread = jnp.concatenate(
            [jnp.broadcast_to(terms[t : t + 1], (POOL, width)) for t in range(tokens)], axis=0
        )
        middle = mid[spot, :].astype(F32) + spread
        mlp_in = rms(middle, gain_m).astype(BF)
        upward = dot(mlp_in, w_up[...])
        activated = gelu(upward)
        res[spot, :] = (middle + dot(activated, w_down[...])).astype(BF)
        return carry

    lax.fori_loop(0, chunks, mlp_chunk, 0)

    def leave(i):
        spot = pl.ds(pl.multiple_of(i * chunk, chunk), chunk)
        return pltpu.make_async_copy(ready.at[spot, :], out.at[spot, :], out_sem.at[i])

    def scatter_chunk(i, carry):
        base = pl.multiple_of(i * chunk, chunk)
        stored = lax.broadcasted_iota(jnp.int32, (chunk, rows), 0) + base
        pick = jnp.where(stored == order[...], 1.0, 0.0).astype(BF)
        ready[pl.ds(base, chunk), :] = dot(pick, res[...]).astype(BF)
        leave(i).start()
        return carry

    lax.fori_loop(0, chunks, scatter_chunk, 0)

    def left(i, carry):
        leave(i).wait()
        return carry

    lax.fori_loop(0, chunks, left, 0)


def on_device(
    sizes,
    points,
    ball_order,
    ball_counts,
    gain_attn,
    gain_mlp,
    head_temps,
    w_qkv,
    w_out,
    c_qkv,
    c_out,
    w_up,
    w_down,
):
    rows, width = points.shape
    heads = head_temps.shape[1]
    seq_n, rep_n = sizes
    peers = seq_n * rep_n
    coarse_rows = rows // POOL
    chunks = rows // (4 * BALL)
    vmem = pl.BlockSpec(memory_space=pltpu.VMEM)
    smem = pl.BlockSpec(memory_space=pltpu.SMEM)
    far = pl.BlockSpec(memory_space=pl.ANY)
    dma = pltpu.SemaphoreType.DMA
    mid, coarse = pl.pallas_call(
        functools.partial(attend_kernel, (*sizes, heads)),
        out_shape=(
            jax.ShapeDtypeStruct((rows, width), BF),
            jax.ShapeDtypeStruct((coarse_rows, width), F32),
        ),
        in_specs=[vmem, vmem, smem, vmem, smem] + [far] * 4,
        out_specs=(far, vmem),
        scratch_shapes=[
            pltpu.VMEM((rows, width), BF),
            pltpu.VMEM((rows, width), BF),
            pltpu.VMEM((rows, width), BF),
            pltpu.VMEM((coarse_rows, width + 128), F32),
            pltpu.VMEM((peers, coarse_rows, width + 128), BF),
            pltpu.VMEM(w_qkv.shape, BF),
            pltpu.VMEM(w_out.shape, BF),
            pltpu.VMEM(c_qkv.shape, BF),
            pltpu.VMEM(c_out.shape, BF),
            dma((4,)),
            dma((chunks,)),
            dma,
            dma((seq_n,)),
            dma((seq_n, rep_n)),
            dma((peers,)),
        ],
        compiler_params=pltpu.CompilerParams(
            collective_id=0, has_side_effects=True, vmem_limit_bytes=VMEM_ATTEND
        ),
        name="attend",
    )(
        points,
        ball_order,
        ball_counts,
        gain_attn.reshape(1, width),
        head_temps,
        w_qkv,
        w_out,
        c_qkv,
        c_out,
    )
    return pl.pallas_call(
        mlp_kernel,
        out_shape=jax.ShapeDtypeStruct(points.shape, points.dtype),
        in_specs=[far, vmem, vmem, vmem, far, far],
        out_specs=far,
        scratch_shapes=[
            pltpu.VMEM((rows, width), BF),
            pltpu.VMEM(w_up.shape, BF),
            pltpu.VMEM(w_down.shape, BF),
            pltpu.VMEM((rows, width), BF),
            pltpu.VMEM((rows, width), BF),
            dma((chunks,)),
            dma((2,)),
            dma((chunks,)),
        ],
        compiler_params=pltpu.CompilerParams(vmem_limit_bytes=VMEM_MLP),
        name="mlp",
    )(mid, coarse, ball_order, gain_mlp.reshape(1, width), w_up, w_down)


def solution(mesh):
    rows = P(("groups", "seq", "rep"))
    sizes = (mesh.shape["seq"], mesh.shape["rep"])
    return jax.shard_map(
        functools.partial(on_device, sizes),
        mesh=mesh,
        in_specs=(P(("groups", "seq", "rep"), None),) * 2 + (rows,) + (P(),) * 9,
        out_specs=P(("groups", "seq", "rep"), None),
        check_vma=False,
    )
```

profile of v0, /device:TPU:0, one launch (start us, length us, event | category | flops | bytes accessed | tf_op | source)
XLA Modules:
  0.0 27.8 jit_solution(5709328080981604722)
XLA Ops:
  0.0 18.2 %attend.1 = (bf16[2048,256]{1,0:T(8,128)(2,1)}, f32[32,256]{1,0:T(8,128)}) custom-call(bf16[2048,256]{1,0:T(8,128)(2,1)} %points.1, s32[1,2048]{1,0:T(1,128)} %order.3, s32[16]{0:T(128)} %counts.1, f32[1,256]{1,0:T(1,128)} %bitcast.2, f32[2,8]{1,0:T(2,128)} %temps.1, bf16[256,768]{1,0:T(8,128)(2,1)} %w_qkv_hbm.1, bf16[256,256]{1,0:T(8,128)(2,1)} %w_out_hbm.1, ...), custom_call_target="tpu_custom_call" | custom-call | tf_op jit(solution)/shard_map/attend/pallas_call | solution.py:413
  18.2 9.6 %mlp.1 = bf16[2048,256]{1,0:T(8,128)(2,1)} custom-call(bf16[2048,256]{1,0:T(8,128)(2,1)} %get-tuple-element.7.mid_hbm, f32[32,256]{1,0:T(8,128)} %get-tuple-element.8.coarse, s32[1,2048]{1,0:T(1,128)} %order.3, f32[1,256]{1,0:T(1,128)} %bitcast.3, bf16[256,1024]{1,0:T(8,128)(2,1)} %w_up_hbm.1, bf16[1024,256]{1,0:T(8,128)(2,1)} %w_down_hbm.1), custom_call_target="tpu_custom_call" | custom-call | tf_op jit(solution)/shard_map/mlp/pallas_call | solution.py:453
where the time goes:
time: 28 us; the launch traced here: 27.8 us
  Pallas kernels  27.8 us (99%)
    pallas_call x1, Pallas kernels, on_device(): pl.pallas_call(functools.partial(attend_kernel, (*sizes, heads)), out_sha...  18.2 us
    pallas_call x1, Pallas kernels, on_device(): pl.pallas_call(mlp_kernel, out_shape=jax.ShapeDtypeStruct(points.shape, p...  9.61 us

commit v1 on v0

--- a/solution.py
+++ b/solution.py
@@ -30,9 +30,9 @@
     return lax.dot_general(a, b, (((1,), (1,)), ((), ())), preferred_element_type=F32)
 
 
-def gelu(upward):
-    inner = upward * (GELU_A + GELU_B * (upward * upward))
-    return (0.5 * upward * (1.0 + jnp.tanh(inner))).astype(BF)
+def gelu_of_half(half):
+    inner = half * (2.0 * GELU_A + 8.0 * GELU_B * (half * half))
+    return half + half * jnp.tanh(inner)
 
 
 def rms(values, gain):
@@ -324,6 +324,9 @@
     w_down,
     res,
     ready,
+    packed,
+    order_twice,
+    spots,
     mid_sem,
     load_sem,
     out_sem,
@@ -332,57 +335,60 @@
     chunk = 4 * BALL
     chunks = rows // chunk
     tokens = chunk // POOL
-    gain_m = gain_mlp[...]
+    gain_half = gain_mlp[...] * 0.5
 
     def enter(i):
-        spot = pl.ds(pl.multiple_of(i * chunk, chunk), chunk)
+        spot = pl.ds(i * chunk, chunk)
         return pltpu.make_async_copy(mid_hbm.at[spot, :], mid.at[spot, :], mid_sem.at[i])
 
+    order_twice[...] = order[...] * 2
     load_up = pltpu.make_async_copy(w_up_hbm, w_up, load_sem.at[0])
     load_down = pltpu.make_async_copy(w_down_hbm, w_down, load_sem.at[1])
+    load_spots = pltpu.make_async_copy(order_twice, spots, load_sem.at[2])
     enter(0).start()
     load_up.start()
     load_down.start()
     for i in range(1, chunks):
         enter(i).start()
+    load_spots.start()
     load_up.wait()
     load_down.wait()
 
-    def mlp_chunk(i, carry):
+    def mlp_chunk(i):
         enter(i).wait()
-        spot = pl.ds(pl.multiple_of(i * chunk, chunk), chunk)
-        terms = coarse[pl.ds(pl.multiple_of(i * tokens, tokens), tokens), :]
+        terms = coarse[pl.ds(i * tokens, tokens), :]
         spread = jnp.concatenate(
             [jnp.broadcast_to(terms[t : t + 1], (POOL, width)) for t in range(tokens)], axis=0
         )
-        middle = mid[spot, :].astype(F32) + spread
-        mlp_in = rms(middle, gain_m).astype(BF)
-        upward = dot(mlp_in, w_up[...])
-        activated = gelu(upward)
-        res[spot, :] = (middle + dot(activated, w_down[...])).astype(BF)
-        return carry
-
-    lax.fori_loop(0, chunks, mlp_chunk, 0)
+        middle = mid[pl.ds(i * chunk, chunk), :].astype(F32) + spread
+        mlp_in = rms(middle, gain_half).astype(BF)
+        activated = gelu_of_half(dot(mlp_in, w_up[...]).astype(BF))
+        result = middle + dot(activated, w_down[...])
+        for n in range(width // LANES):
+            res[pl.ds(2 * i * chunk + n, chunk, stride=2), :] = result[:, n * LANES : (n + 1) * LANES]
+
+    def scatter_chunk(i):
+        for r in range(i * chunk, (i + 1) * chunk):
+            ready[pl.ds(spots[0, r], 2), :] = res[pl.ds(2 * r, 2), :]
+
+    mlp_chunk(0)
+    load_spots.wait()
+    for i in range(1, chunks):
+        scatter_chunk(i - 1)
+        mlp_chunk(i)
+    scatter_chunk(chunks - 1)
 
     def leave(i):
-        spot = pl.ds(pl.multiple_of(i * chunk, chunk), chunk)
-        return pltpu.make_async_copy(ready.at[spot, :], out.at[spot, :], out_sem.at[i])
-
-    def scatter_chunk(i, carry):
-        base = pl.multiple_of(i * chunk, chunk)
-        stored = lax.broadcasted_iota(jnp.int32, (chunk, rows), 0) + base
-        pick = jnp.where(stored == order[...], 1.0, 0.0).astype(BF)
-        ready[pl.ds(base, chunk), :] = dot(pick, res[...]).astype(BF)
+        spot = pl.ds(i * chunk, chunk)
+        return pltpu.make_async_copy(packed.at[spot, :], out.at[spot, :], out_sem.at[i])
+
+    for i in range(chunks):
+        packed[pl.ds(i * chunk, chunk), :] = jnp.concatenate(
+            [ready[pl.ds(2 * i * chunk + n, chunk, stride=2), :] for n in range(width // LANES)], axis=1
+        ).astype(BF)
         leave(i).start()
-        return carry
-
-    lax.fori_loop(0, chunks, scatter_chunk, 0)
-
-    def left(i, carry):
+    for i in range(chunks):
         leave(i).wait()
-        return carry
-
-    lax.fori_loop(0, chunks, left, 0)
 
 
 def on_device(
@@ -459,10 +465,13 @@
             pltpu.VMEM((rows, width), BF),
             pltpu.VMEM(w_up.shape, BF),
             pltpu.VMEM(w_down.shape, BF),
+            pltpu.VMEM((rows * width // LANES, LANES), F32),
+            pltpu.VMEM((rows * width // LANES, LANES), F32),
             pltpu.VMEM((rows, width), BF),
-            pltpu.VMEM((rows, width), BF),
+            pltpu.VMEM((1, rows), jnp.int32),
+            pltpu.SMEM((1, rows), jnp.int32),
             dma((chunks,)),
-            dma((2,)),
+            dma((3,)),
             dma((chunks,)),
         ],
         compiler_params=pltpu.CompilerParams(vmem_limit_bytes=VMEM_MLP),

time: 28 us -> 25.9 us (0.925)
  Pallas kernels: 27.8 us -> 25.7 us
    pallas_call x1, Pallas kernels: 9.61 us -> 7.53 us  [on_device(): pl.pallas_call(mlp_kernel, out_shape=jax.ShapeDtypeStruct(points.shape, p...]
where the time goes in v1:
time: 25.9 us; the launch traced here: 25.7 us
  Pallas kernels  25.7 us (99%)
    pallas_call x1, Pallas kernels, on_device(): pl.pallas_call(functools.partial(attend_kernel, (*sizes, heads)), out_sha...  18.2 us
    pallas_call x1, Pallas kernels, on_device(): pl.pallas_call(mlp_kernel, out_shape=jax.ShapeDtypeStruct(points.shape, p...  7.53 us

profile of v1, /device:TPU:0, one launch (start us, length us, event | category | flops | bytes accessed | tf_op | source)
XLA Modules:
  0.0 25.7 jit_solution(8722804824903327084)
XLA Ops:
  0.0 18.2 %attend.1 = (bf16[2048,256]{1,0:T(8,128)(2,1)}, f32[32,256]{1,0:T(8,128)}) custom-call(bf16[2048,256]{1,0:T(8,128)(2,1)} %points.1, s32[1,2048]{1,0:T(1,128)} %order.3, s32[16]{0:T(128)} %counts.1, f32[1,256]{1,0:T(1,128)} %bitcast.2, f32[2,8]{1,0:T(2,128)} %temps.1, bf16[256,768]{1,0:T(8,128)(2,1)} %w_qkv_hbm.1, bf16[256,256]{1,0:T(8,128)(2,1)} %w_out_hbm.1, ...), custom_call_target="tpu_custom_call" | custom-call | tf_op jit(solution)/shard_map/attend/pallas_call | solution.py:419
  18.2 7.5 %mlp.1 = bf16[2048,256]{1,0:T(8,128)(2,1)} custom-call(bf16[2048,256]{1,0:T(8,128)(2,1)} %get-tuple-element.7.mid_hbm, f32[32,256]{1,0:T(8,128)} %get-tuple-element.8.coarse, s32[1,2048]{1,0:T(1,128)} %order.3, f32[1,256]{1,0:T(1,128)} %bitcast.3, bf16[256,1024]{1,0:T(8,128)(2,1)} %w_up_hbm.1, bf16[1024,256]{1,0:T(8,128)(2,1)} %w_down_hbm.1), custom_call_target="tpu_custom_call" | custom-call | tf_op jit(solution)/shard_map/mlp/pallas_call | solution.py:459

commit v2 on v1

--- a/solution.py
+++ b/solution.py
@@ -11,11 +11,12 @@
 BALL = 128
 POOL = 64
 EPS = 1e-06
-VMEM_ATTEND = 61 << 20
-VMEM_MLP = 61 << 20
+VMEM_ATTEND = 32 << 20
+VMEM_MLP = 32 << 20
 LANES = 128
 GELU_A = math.sqrt(2.0 / math.pi)
 GELU_B = 0.044715 * math.sqrt(2.0 / math.pi)
+NO_TOKEN = 1024.0
 LOG2E = 1.4426950408889634
 MESH = pl.DeviceIdType.MESH
 BF = jnp.bfloat16
@@ -41,29 +42,36 @@
 
 def attend_kernel(
     sizes,
-    points,
-    order,
-    counts,
-    gain_attn,
-    temps,
+    points_hbm,
+    order_hbm,
+    counts_hbm,
+    gain_hbm,
+    temps_hbm,
     w_qkv_hbm,
     w_out_hbm,
     c_qkv_hbm,
     c_out_hbm,
-    mid_out,
+    mid,
     coarse,
+    points,
+    order,
+    order_twice,
+    gain_attn,
+    spots,
+    counts,
+    temps,
+    wide,
+    picked,
     srt,
     nrm,
-    mid,
     stage,
     tokens_all,
     w_qkv,
     w_out,
     c_qkv,
     c_out,
+    points_sem,
     load_sem,
-    out_sem,
-    local_sem,
     seq_send,
     rep_send,
     recv_sem,
@@ -76,17 +84,33 @@
     chunks = rows // chunk
     tokens = chunk // POOL
     coarse_rows = rows // POOL
+    halves = width // LANES
     my_seq = lax.axis_index("seq")
     my_rep = lax.axis_index("rep")
     me = my_seq * rep_n + my_rep
 
-    loads = [
+    small = [
         pltpu.make_async_copy(source, target, load_sem.at[n])
         for n, (source, target) in enumerate(
+            [(order_hbm, order), (counts_hbm, counts), (temps_hbm, temps), (gain_hbm, gain_attn)]
+        )
+    ]
+    loads = [
+        pltpu.make_async_copy(source, target, load_sem.at[4 + n])
+        for n, (source, target) in enumerate(
             [(w_qkv_hbm, w_qkv), (w_out_hbm, w_out), (c_qkv_hbm, c_qkv), (c_out_hbm, c_out)]
         )
     ]
-    for load in loads:
+    load_spots = pltpu.make_async_copy(order_twice, spots, load_sem.at[8])
+
+    def enter(i):
+        spot = pl.ds(i * chunk, chunk)
+        return pltpu.make_async_copy(points_hbm.at[spot, :], points.at[spot, :], points_sem.at[i])
+
+    small[0].start()
+    for i in range(chunks):
+        enter(i).start()
+    for load in small[1:] + loads:
         load.start()
 
     barrier = pltpu.get_barrier_semaphore()
@@ -103,6 +127,10 @@
 
     lax.fori_loop(1, seq_n, greet_seq, 0)
     lax.fori_loop(1, rep_n, greet_rep, 0)
+
+    small[0].wait()
+    order_twice[...] = order[...] * 2
+    load_spots.start()
 
     lane_head = lax.broadcasted_iota(jnp.int32, (1, width), 1) // head_dim
     near_heads = LANES // head_dim
@@ -129,28 +157,29 @@
     def head_rms(values):
         return values * lax.rsqrt(dot((values * values).astype(BF), block_mean) + EPS)
 
+    for i in range(chunks):
+        enter(i).wait()
+        block = points[pl.ds(i * chunk, chunk), :].astype(F32)
+        for n in range(halves):
+            wide[pl.ds(2 * i * chunk + n, chunk, stride=2), :] = block[:, slabs[n]]
+    for load in small[1:]:
+        load.wait()
+    load_spots.wait()
+
     gain_a = gain_attn[...]
 
-    def gather_chunk(i, carry):
-        base = pl.multiple_of(i * chunk, chunk)
-        picks = []
-        lane = lax.broadcasted_iota(jnp.int32, (BALL, BALL), 1).astype(F32)
-        for b in range(4):
-            row = order[:, pl.ds(base + b * BALL, BALL)].astype(F32)
-            column = jnp.transpose(jnp.broadcast_to(row, (BALL, BALL)))
-            picks.append(
-                jnp.concatenate(
-                    [
-                        jnp.where(column == lane + float(j * BALL), 1.0, 0.0).astype(BF)
-                        for j in range(rows // BALL)
-                    ],
-                    axis=1,
-                )
-            )
-        sorted_rows = dot(jnp.concatenate(picks, axis=0), points[...])
-        srt[pl.ds(base, chunk), :] = sorted_rows.astype(BF)
+    def gather_chunk(i):
+        for r in range(i * chunk, (i + 1) * chunk):
+            picked[pl.ds(2 * r, 2), :] = wide[pl.ds(spots[0, r], 2), :]
+
+    def pool_chunk(i):
+        sorted_rows = jnp.concatenate(
+            [picked[pl.ds(2 * i * chunk + n, chunk, stride=2), :] for n in range(halves)], axis=1
+        )
+        spot = pl.ds(i * chunk, chunk)
+        srt[spot, :] = sorted_rows.astype(BF)
         normed = rms(sorted_rows, gain_a).astype(BF)
-        nrm[pl.ds(base, chunk), :] = normed
+        nrm[spot, :] = normed
         shape = (2 * tokens, chunk)
         token = lax.broadcasted_iota(jnp.int32, shape, 0)
         place = lax.broadcasted_iota(jnp.int32, shape, 1)
@@ -162,17 +191,27 @@
         take = jnp.where((offset >= 0) & (offset < half), 1.0, 0.0).astype(BF)
         total = dot(take, normed)[:tokens]
         half_f = half[:tokens, :width].astype(F32)
-        spot = pl.ds(pl.multiple_of(i * tokens, tokens), tokens)
-        stage[spot, :width] = total / jnp.maximum(half_f, 1.0)
-        stage[spot, width:] = jnp.where(half_f[:, :128] > 0.0, 1.0, 0.0)
-        return carry
-
-    lax.fori_loop(0, chunks, gather_chunk, 0)
+        stage[pl.ds(i * tokens, tokens), :] = jnp.where(
+            half_f > 0.0, total / jnp.maximum(half_f, 1.0), NO_TOKEN
+        )
+
+    gather_chunk(0)
+    for i in range(1, chunks):
+        gather_chunk(i)
+        pool_chunk(i - 1)
+    pool_chunk(chunks - 1)
 
     own_block = stage[...].astype(BF)
     tokens_all[me] = own_block
 
     pl.semaphore_wait(barrier, seq_n + rep_n - 2)
+
+    def seq_place(step):
+        low = my_seq < seq_n // 2
+        above = seq_n - 1 - my_seq
+        rising = jnp.where(step < above, seq_n - 1 - step, step - above)
+        falling = jnp.where(step < my_seq, step, seq_n - 1 - step + my_seq)
+        return jnp.where(low, rising, falling)
 
     def seq_copy(step):
         return pltpu.make_async_remote_copy(
@@ -180,16 +219,16 @@
             dst_ref=tokens_all.at[me],
             send_sem=seq_send.at[step],
             recv_sem=recv_sem.at[me],
-            device_id={"seq": lax.rem(my_seq + step, seq_n), "rep": my_rep},
+            device_id={"seq": seq_place(step), "rep": my_rep},
             device_id_type=MESH,
         )
 
-    def rep_copy(away, step):
-        block = lax.rem(my_seq + away, seq_n) * rep_n + my_rep
+    def rep_copy(block_seq, step):
+        block = block_seq * rep_n + my_rep
         return pltpu.make_async_remote_copy(
             src_ref=tokens_all.at[block],
             dst_ref=tokens_all.at[block],
-            send_sem=rep_send.at[away, step],
+            send_sem=rep_send.at[block_seq, step],
             recv_sem=recv_sem.at[block],
             device_id={"seq": my_seq, "rep": lax.rem(my_rep + step, rep_n)},
             device_id_type=MESH,
@@ -212,12 +251,13 @@
 
         lax.fori_loop(first, count, body, 0)
 
-    each(seq_n, 1, lambda step: seq_copy(step).start())
-    each(rep_n, 1, lambda step: rep_copy(0, step).start())
-
-    def relay(away):
-        arrival(lax.rem(my_seq + away, seq_n) * rep_n + my_rep).wait_recv()
-        each(rep_n, 1, lambda step: rep_copy(away, step).start())
+    each(seq_n - 1, 0, lambda step: seq_copy(step).start())
+    each(rep_n, 1, lambda step: rep_copy(my_seq, step).start())
+
+    def relay(step):
+        place = seq_place(seq_n - 2 - step)
+        arrival(place * rep_n + my_rep).wait_recv()
+        each(rep_n, 1, lambda away: rep_copy(place, away).start())
 
     for load in loads:
         load.wait()
@@ -247,21 +287,20 @@
         mid[spot, :] = (srt[spot, :].astype(F32) + fine).astype(BF)
         return carry
 
-    def leave(i):
-        spot = pl.ds(pl.multiple_of(i * chunk, chunk), chunk)
-        return pltpu.make_async_copy(mid.at[spot, :], mid_out.at[spot, :], out_sem.at[i])
-
     def ball_step(i, carry):
         ball_chunk(i, carry)
-        leave(i).start()
         return carry
 
     early = chunks // 2
+    first = (seq_n - 1) // 2
     lax.fori_loop(0, early, ball_step, 0)
-    each(seq_n, 1, relay)
-    lax.fori_loop(early, chunks, ball_step, 0)
-
-    q_c = dot(own_block[:, :width], c_qkv[:, :width])
+    each(first, 0, relay)
+    lax.fori_loop(early, chunks - 1, ball_step, 0)
+    each(seq_n - 1, first, relay)
+    lax.fori_loop(chunks - 1, chunks, ball_step, 0)
+
+    own_tokens = jnp.where(own_block < NO_TOKEN / 2, own_block, 0.0).astype(BF)
+    q_c = dot(own_tokens, c_qkv[:, :width])
     q_c = (head_rms(q_c) * lane_scale(1)).astype(BF)
     queries = [by_head(q_c[:, slab]) for slab in slabs]
 
@@ -277,14 +316,16 @@
     group = math.gcd(peers, 16)
 
     def coarse_keys(g):
-        block = tokens_all[pl.ds(g * group, group)].reshape(group * coarse_rows, width + 128)
-        joined = dot(block[:, :width], c_qkv[:, width:])
+        block = tokens_all[pl.ds(g * group, group)].reshape(group * coarse_rows, width)
+        there = block < NO_TOKEN / 2
+        ones = jnp.where(there[:, :LANES], 1.0, 0.0).astype(BF)
+        joined = dot(jnp.where(there, block, 0.0).astype(BF), c_qkv[:, width:])
         keys = head_rms(joined[:, :width]).astype(BF)
         values = joined[:, width:].astype(BF)
         sums = []
         for query, slab in zip(queries, slabs):
             weights = jnp.exp2(dot_t(query, keys[:, slab])).astype(BF)
-            sums.append(dot(weights, jnp.concatenate([values[:, slab], block[:, width:]], axis=1)))
+            sums.append(dot(weights, jnp.concatenate([values[:, slab], ones], axis=1)))
         return sums
 
     if peers == group:
@@ -306,9 +347,8 @@
     mix = jnp.concatenate(slab_mixes, axis=1)
     coarse[...] = dot(mix.astype(BF), c_out[...])
 
-    each(seq_n, 1, lambda step: seq_copy(step).wait_send())
+    each(seq_n - 1, 0, lambda step: seq_copy(step).wait_send())
     each(seq_n, 0, lambda away: each(rep_n, 1, lambda step: rep_copy(away, step).wait_send()))
-    each(chunks, 0, lambda i: leave(i).wait())
 
 
 def mlp_kernel(
@@ -355,7 +395,6 @@
     load_down.wait()
 
     def mlp_chunk(i):
-        enter(i).wait()
         terms = coarse[pl.ds(i * tokens, tokens), :]
         spread = jnp.concatenate(
             [jnp.broadcast_to(terms[t : t + 1], (POOL, width)) for t in range(tokens)], axis=0
@@ -371,7 +410,10 @@
         for r in range(i * chunk, (i + 1) * chunk):
             ready[pl.ds(spots[0, r], 2), :] = res[pl.ds(2 * r, 2), :]
 
+    enter(0).wait()
     mlp_chunk(0)
+    for i in range(1, chunks):
+        enter(i).wait()
     load_spots.wait()
     for i in range(1, chunks):
         scatter_chunk(i - 1)
@@ -413,30 +455,38 @@
     coarse_rows = rows // POOL
     chunks = rows // (4 * BALL)
     vmem = pl.BlockSpec(memory_space=pltpu.VMEM)
-    smem = pl.BlockSpec(memory_space=pltpu.SMEM)
+    hbm = pl.BlockSpec(memory_space=pltpu.HBM)
     far = pl.BlockSpec(memory_space=pl.ANY)
     dma = pltpu.SemaphoreType.DMA
+    tall = rows * width // LANES
     mid, coarse = pl.pallas_call(
         functools.partial(attend_kernel, (*sizes, heads)),
         out_shape=(
             jax.ShapeDtypeStruct((rows, width), BF),
             jax.ShapeDtypeStruct((coarse_rows, width), F32),
         ),
-        in_specs=[vmem, vmem, smem, vmem, smem] + [far] * 4,
-        out_specs=(far, vmem),
+        in_specs=[hbm] * 9,
+        out_specs=(vmem, vmem),
         scratch_shapes=[
             pltpu.VMEM((rows, width), BF),
+            pltpu.VMEM((1, rows), jnp.int32),
+            pltpu.VMEM((1, rows), jnp.int32),
+            pltpu.VMEM((1, width), F32),
+            pltpu.SMEM((1, rows), jnp.int32),
+            pltpu.SMEM(ball_counts.shape, jnp.int32),
+            pltpu.SMEM(head_temps.shape, F32),
+            pltpu.VMEM((tall, LANES), F32),
+            pltpu.VMEM((tall, LANES), F32),
             pltpu.VMEM((rows, width), BF),
             pltpu.VMEM((rows, width), BF),
-            pltpu.VMEM((coarse_rows, width + 128), F32),
-            pltpu.VMEM((peers, coarse_rows, width + 128), BF),
+            pltpu.VMEM((coarse_rows, width), F32),
+            pltpu.VMEM((peers, coarse_rows, width), BF),
             pltpu.VMEM(w_qkv.shape, BF),
             pltpu.VMEM(w_out.shape, BF),
             pltpu.VMEM(c_qkv.shape, BF),
             pltpu.VMEM(c_out.shape, BF),
-            dma((4,)),
             dma((chunks,)),
-            dma,
+            dma((9,)),
             dma((seq_n,)),
             dma((seq_n, rep_n)),
             dma((peers,)),

time: 25.9 us -> 27.9 us (1.077)
  local copies, waits for them, and re-layouts: 0 us -> 7.08 us
  Pallas kernels: 25.7 us -> 20.4 us
    unnamed x0 -> x24, local copies, waits for them, and re-layouts: none -> 7.08 us
    pallas_call x1, Pallas kernels: 7.53 us -> 4.69 us  [on_device(): pl.pallas_call(mlp_kernel, out_shape=jax.ShapeDtypeStruct(points.shape, p...]
    pallas_call x1, Pallas kernels: 18.2 us -> 15.7 us  [on_device(): pl.pallas_call(functools.partial(attend_kernel, (*sizes, heads)), out_sha...]
where the time goes in v2:
time: 27.9 us; the launch traced here: 27.5 us
  Pallas kernels  20.4 us (73%)
  local copies, waits for them, and re-layouts  7.08 us (25%)
    pallas_call x1, Pallas kernels, on_device(): pl.pallas_call(functools.partial(attend_kernel, (*sizes, heads)), out_sha...  15.7 us
    unnamed x24, local copies, waits for them, and re-layouts  7.08 us
    pallas_call x1, Pallas kernels, on_device(): pl.pallas_call(mlp_kernel, out_shape=jax.ShapeDtypeStruct(points.shape, p...  4.69 us

profile of v2, /device:TPU:0, one launch (start us, length us, event | category | flops | bytes accessed | tf_op | source)
XLA Modules:
  0.0 27.5 jit_solution(13402886797179248357)
XLA Ops:
  0.0 0.0 copy-start.9
  0.0 0.0 copy-start.8
  0.0 0.0 copy-start.11
  0.0 0.7 %copy-done.9 = f32[2,8]{1,0:T(2,128)S(1)} copy-done((f32[2,8]{1,0:T(2,128)S(1)}, f32[2,8]{1,0:T(2,128)}, u32[]{:S(2)}) %copy-start.9) | copy-done | bytes 88
  0.7 0.0 copy-done.8
  0.7 0.0 copy-done.11
  0.7 0.0 copy-start
  0.7 1.2 %copy-done = bf16[2048,256]{1,0:T(8,128)(2,1)S(1)} copy-done((bf16[2048,256]{1,0:T(8,128)(2,1)S(1)}, bf16[2048,256]{1,0:T(8,128)(2,1)}, u32[]{:S(2)}) %copy-start) | copy-done | bytes 1048600
  1.9 0.0 copy-start.3
  1.9 1.0 %copy-done.3 = bf16[256,768]{1,0:T(8,128)(2,1)S(1)} copy-done((bf16[256,768]{1,0:T(8,128)(2,1)S(1)}, bf16[256,768]{1,0:T(8,128)(2,1)}, u32[]{:S(2)}) %copy-start.3) | copy-done | bytes 393240
  2.9 0.0 copy-start.4
  2.9 1.0 %copy-done.4 = bf16[256,768]{1,0:T(8,128)(2,1)S(1)} copy-done((bf16[256,768]{1,0:T(8,128)(2,1)S(1)}, bf16[256,768]{1,0:T(8,128)(2,1)}, u32[]{:S(2)}) %copy-start.4) | copy-done | bytes 393240
  3.9 0.0 copy-start.5
  3.9 0.9 %copy-done.5 = bf16[256,256]{1,0:T(8,128)(2,1)S(1)} copy-done((bf16[256,256]{1,0:T(8,128)(2,1)S(1)}, bf16[256,256]{1,0:T(8,128)(2,1)}, u32[]{:S(2)}) %copy-start.5) | copy-done | bytes 131096
  4.8 0.0 copy-start.6
  4.8 0.9 %copy-done.6 = bf16[256,256]{1,0:T(8,128)(2,1)S(1)} copy-done((bf16[256,256]{1,0:T(8,128)(2,1)S(1)}, bf16[256,256]{1,0:T(8,128)(2,1)}, u32[]{:S(2)}) %copy-start.6) | copy-done | bytes 131096
  5.7 0.0 copy-start.7
  5.7 0.7 %copy-done.7 = s32[1,2048]{1,0:T(1,128)S(1)} copy-done((s32[1,2048]{1,0:T(1,128)S(1)}, s32[1,2048]{1,0:T(1,128)}, u32[]{:S(2)}) %copy-start.7) | copy-done | bytes 8216
  6.4 0.0 copy-start.1
  6.4 0.0 copy-start.2
  6.4 15.7 %attend.1 = (bf16[2048,256]{1,0:T(8,128)(2,1)S(1)}, f32[32,256]{1,0:T(8,128)S(1)}) custom-call(bf16[2048,256]{1,0:T(8,128)(2,1)S(1)} %copy-done, s32[1,2048]{1,0:T(1,128)S(1)} %copy-done.7, s32[16]{0:T(128)S(1)} %copy-done.11, f32[1,256]{1,0:T(1,128)S(1)} %bitcast.2, f32[2,8]{1,0:T(2,128)S(1)} %copy-done.9, bf16[256,768]{1,0:T(8,128)(2,1)S(1)} %copy-done.3, ...), custom_call_target="tpu_custom_call" | custom-call | tf_op jit(solution)/shard_map/attend/pallas_call | solution.py:462
  22.2 0.0 copy-start.10
  22.2 0.0 copy-done.1
  22.2 0.0 copy-done.2
  22.2 0.7 %copy-done.10 = f32[256]{0:T(256)S(1)} copy-done((f32[256]{0:T(256)S(1)}, f32[256]{0:T(256)}, u32[]{:S(2)}) %copy-start.10) | copy-done | bytes 1048
  22.8 4.7 %mlp.1 = bf16[2048,256]{1,0:T(8,128)(2,1)} custom-call(bf16[2048,256]{1,0:T(8,128)(2,1)S(1)} %get-tuple-element.7.mid_hbm, f32[32,256]{1,0:T(8,128)S(1)} %get-tuple-element.8.coarse, s32[1,2048]{1,0:T(1,128)S(1)} %copy-done.7, f32[1,256]{1,0:T(1,128)S(1)} %bitcast.3, bf16[256,1024]{1,0:T(8,128)(2,1)S(1)} %copy-done.1, bf16[1024,256]{1,0:T(8,128)(2,1)S(1)} %copy-done.2), custom_call_target="tpu_custom_call" | custom-call | tf_op jit(solution)/shard_map/mlp/pallas_call | solution.py:509
Async XLA Ops:
  0.0 0.7 %copy-start.9 = (f32[2,8]{1,0:T(2,128)S(1)}, f32[2,8]{1,0:T(2,128)}, u32[]{:S(2)}) copy-start(f32[2,8]{1,0:T(2,128)} %temps_hbm.1) | copy-start | bytes 196
  0.0 0.7 %copy-start.8 = (f32[256]{0:T(256)S(1)}, f32[256]{0:T(256)}, u32[]{:S(2)}) copy-start(f32[256]{0:T(256)} %param.15) | copy-start | bytes 3076
  0.0 0.7 %copy-start.11 = (s32[16]{0:T(128)S(1)}, s32[16]{0:T(128)}, u32[]{:S(2)}) copy-start(s32[16]{0:T(128)} %counts_hbm.1) | copy-start | bytes 196
  0.7 1.2 %copy-start = (bf16[2048,256]{1,0:T(8,128)(2,1)S(1)}, bf16[2048,256]{1,0:T(8,128)(2,1)}, u32[]{:S(2)}) copy-start(bf16[2048,256]{1,0:T(8,128)(2,1)} %points_hbm.1) | copy-start | bytes 3145732
  1.9 1.0 %copy-start.3 = (bf16[256,768]{1,0:T(8,128)(2,1)S(1)}, bf16[256,768]{1,0:T(8,128)(2,1)}, u32[]{:S(2)}) copy-start(bf16[256,768]{1,0:T(8,128)(2,1)} %w_qkv_hbm.1) | copy-start | bytes 1179652
  2.9 1.0 %copy-start.4 = (bf16[256,768]{1,0:T(8,128)(2,1)S(1)}, bf16[256,768]{1,0:T(8,128)(2,1)}, u32[]{:S(2)}) copy-start(bf16[256,768]{1,0:T(8,128)(2,1)} %c_qkv_hbm.1) | copy-start | bytes 1179652
  3.9 0.9 %copy-start.5 = (bf16[256,256]{1,0:T(8,128)(2,1)S(1)}, bf16[256,256]{1,0:T(8,128)(2,1)}, u32[]{:S(2)}) copy-start(bf16[256,256]{1,0:T(8,128)(2,1)} %w_out_hbm.1) | copy-start | bytes 393220
  4.8 0.9 %copy-start.6 = (bf16[256,256]{1,0:T(8,128)(2,1)S(1)}, bf16[256,256]{1,0:T(8,128)(2,1)}, u32[]{:S(2)}) copy-start(bf16[256,256]{1,0:T(8,128)(2,1)} %c_out_hbm.1) | copy-start | bytes 393220
  5.7 0.7 %copy-start.7 = (s32[1,2048]{1,0:T(1,128)S(1)}, s32[1,2048]{1,0:T(1,128)}, u32[]{:S(2)}) copy-start(s32[1,2048]{1,0:T(1,128)} %order.1) | copy-start | bytes 24580
  6.4 15.8 %copy-start.1 = (bf16[256,1024]{1,0:T(8,128)(2,1)S(1)}, bf16[256,1024]{1,0:T(8,128)(2,1)}, u32[]{:S(2)}) copy-start(bf16[256,1024]{1,0:T(8,128)(2,1)} %w_up_hbm.1) | copy-start | bytes 1572868
  6.4 15.8 %copy-start.2 = (bf16[1024,256]{1,0:T(8,128)(2,1)S(1)}, bf16[1024,256]{1,0:T(8,128)(2,1)}, u32[]{:S(2)}) copy-start(bf16[1024,256]{1,0:T(8,128)(2,1)} %w_down_hbm.1) | copy-start | bytes 1572868
  22.2 0.7 %copy-start.10 = (f32[256]{0:T(256)S(1)}, f32[256]{0:T(256)}, u32[]{:S(2)}) copy-start(f32[256]{0:T(256)} %param.16) | copy-start | bytes 3076

commit v3 on v2

--- a/solution.py
+++ b/solution.py
@@ -51,8 +51,10 @@
     w_out_hbm,
     c_qkv_hbm,
     c_out_hbm,
+    gain_mlp_hbm,
     mid,
     coarse,
+    gain_mid,
     points,
     order,
     order_twice,
@@ -98,10 +100,16 @@
     loads = [
         pltpu.make_async_copy(source, target, load_sem.at[4 + n])
         for n, (source, target) in enumerate(
-            [(w_qkv_hbm, w_qkv), (w_out_hbm, w_out), (c_qkv_hbm, c_qkv), (c_out_hbm, c_out)]
+            [
+                (w_qkv_hbm, w_qkv),
+                (w_out_hbm, w_out),
+                (c_qkv_hbm, c_qkv),
+                (c_out_hbm, c_out),
+                (gain_mlp_hbm, gain_mid),
+            ]
         )
     ]
-    load_spots = pltpu.make_async_copy(order_twice, spots, load_sem.at[8])
+    load_spots = pltpu.make_async_copy(order_twice, spots, load_sem.at[9])
 
     def enter(i):
         spot = pl.ds(i * chunk, chunk)
@@ -352,22 +360,18 @@
 
 
 def mlp_kernel(
-    mid_hbm,
+    mid,
     coarse,
     order,
     gain_mlp,
-    w_up_hbm,
-    w_down_hbm,
-    out,
-    mid,
     w_up,
     w_down,
+    out,
     res,
     ready,
     packed,
     order_twice,
     spots,
-    mid_sem,
     load_sem,
     out_sem,
 ):
@@ -377,22 +381,9 @@
     tokens = chunk // POOL
     gain_half = gain_mlp[...] * 0.5
 
-    def enter(i):
-        spot = pl.ds(i * chunk, chunk)
-        return pltpu.make_async_copy(mid_hbm.at[spot, :], mid.at[spot, :], mid_sem.at[i])
-
     order_twice[...] = order[...] * 2
-    load_up = pltpu.make_async_copy(w_up_hbm, w_up, load_sem.at[0])
-    load_down = pltpu.make_async_copy(w_down_hbm, w_down, load_sem.at[1])
-    load_spots = pltpu.make_async_copy(order_twice, spots, load_sem.at[2])
-    enter(0).start()
-    load_up.start()
-    load_down.start()
-    for i in range(1, chunks):
-        enter(i).start()
+    load_spots = pltpu.make_async_copy(order_twice, spots, load_sem)
     load_spots.start()
-    load_up.wait()
-    load_down.wait()
 
     def mlp_chunk(i):
         terms = coarse[pl.ds(i * tokens, tokens), :]
@@ -410,10 +401,7 @@
         for r in range(i * chunk, (i + 1) * chunk):
             ready[pl.ds(spots[0, r], 2), :] = res[pl.ds(2 * r, 2), :]
 
-    enter(0).wait()
     mlp_chunk(0)
-    for i in range(1, chunks):
-        enter(i).wait()
     load_spots.wait()
     for i in range(1, chunks):
         scatter_chunk(i - 1)
@@ -459,14 +447,15 @@
     far = pl.BlockSpec(memory_space=pl.ANY)
     dma = pltpu.SemaphoreType.DMA
     tall = rows * width // LANES
-    mid, coarse = pl.pallas_call(
+    mid, coarse, gain_mid = pl.pallas_call(
         functools.partial(attend_kernel, (*sizes, heads)),
         out_shape=(
             jax.ShapeDtypeStruct((rows, width), BF),
             jax.ShapeDtypeStruct((coarse_rows, width), F32),
+            jax.ShapeDtypeStruct((1, width), F32),
         ),
-        in_specs=[hbm] * 9,
-        out_specs=(vmem, vmem),
+        in_specs=[hbm] * 10,
+        out_specs=(vmem,) * 3,
         scratch_shapes=[
             pltpu.VMEM((rows, width), BF),
             pltpu.VMEM((1, rows), jnp.int32),
@@ -486,7 +475,7 @@
             pltpu.VMEM(c_qkv.shape, BF),
             pltpu.VMEM(c_out.shape, BF),
             dma((chunks,)),
-            dma((9,)),
+            dma((10,)),
             dma((seq_n,)),
             dma((seq_n, rep_n)),
             dma((peers,)),
@@ -496,37 +485,39 @@
         ),
         name="attend",
     )(
-        points,
-        ball_order,
-        ball_counts,
-        gain_attn.reshape(1, width),
-        head_temps,
-        w_qkv,
-        w_out,
-        c_qkv,
-        c_out,
+        *(
+            pltpu.with_memory_space_constraint(operand, pltpu.HBM)
+            for operand in (
+                points,
+                ball_order,
+                ball_counts,
+                gain_attn.reshape(1, width),
+                head_temps,
+                w_qkv,
+                w_out,
+                c_qkv,
+                c_out,
+                gain_mlp.reshape(1, width),
+            )
+        )
     )
     return pl.pallas_call(
         mlp_kernel,
         out_shape=jax.ShapeDtypeStruct(points.shape, points.dtype),
-        in_specs=[far, vmem, vmem, vmem, far, far],
+        in_specs=[vmem] * 6,
         out_specs=far,
         scratch_shapes=[
-            pltpu.VMEM((rows, width), BF),
-            pltpu.VMEM(w_up.shape, BF),
-            pltpu.VMEM(w_down.shape, BF),
-            pltpu.VMEM((rows * width // LANES, LANES), F32),
-            pltpu.VMEM((rows * width // LANES, LANES), F32),
+            pltpu.VMEM((tall, LANES), F32),
+            pltpu.VMEM((tall, LANES), F32),
             pltpu.VMEM((rows, width), BF),
             pltpu.VMEM((1, rows), jnp.int32),
             pltpu.SMEM((1, rows), jnp.int32),
-            dma((chunks,)),
-            dma((3,)),
+            dma,
             dma((chunks,)),
         ],
         compiler_params=pltpu.CompilerParams(vmem_limit_bytes=VMEM_MLP),
         name="mlp",
-    )(mid, coarse, ball_order, gain_mlp.reshape(1, width), w_up, w_down)
+    )(mid, coarse, ball_order, gain_mid, w_up, w_down)
 
 
 def solution(mesh):

time: 27.9 us -> 20.5 us (0.73)
  local copies, waits for them, and re-layouts: 7.08 us -> 0.01 us
    unnamed x24 -> x6, local copies, waits for them, and re-layouts: 7.08 us -> 0.01 us
    pallas_call x1, Pallas kernels: 15.7 us -> 15.2 us  [on_device(): pl.pallas_call(functools.partial(attend_kernel, (*sizes, heads)), out_sha...]
    pallas_call x1, Pallas kernels: 4.69 us -> 5.09 us  [on_device(): pl.pallas_call(mlp_kernel, out_shape=jax.ShapeDtypeStruct(points.shape, p...]
where the time goes in v3:
time: 20.5 us; the launch traced here: 20.4 us
  Pallas kernels  20.3 us (99%)
    pallas_call x1, Pallas kernels, on_device(): pl.pallas_call(functools.partial(attend_kernel, (*sizes, heads)), out_sha...  15.2 us
    pallas_call x1, Pallas kernels, on_device(): pl.pallas_call(mlp_kernel, out_shape=jax.ShapeDtypeStruct(points.shape, p...  5.09 us

profile of v3, /device:TPU:0, one launch (start us, length us, event | category | flops | bytes accessed | tf_op | source)
XLA Modules:
  0.0 20.4 jit_solution(10646514427508521113)
XLA Ops:
  0.0 0.0 copy-start
  0.0 0.0 copy-start.1
  0.0 0.0 copy-start.2
  0.0 15.2 %attend.1 = (bf16[2048,256]{1,0:T(8,128)(2,1)S(1)}, f32[32,256]{1,0:T(8,128)S(1)}, f32[1,256]{1,0:T(1,128)S(1)}) custom-call(bf16[2048,256]{1,0:T(8,128)(2,1)} %points_hbm.1, s32[1,2048]{1,0:T(1,128)} %order.1, s32[16]{0:T(128)} %counts_hbm.1, f32[1,256]{1,0:T(1,128)} %bitcast.2, f32[2,8]{1,0:T(2,128)} %temps_hbm.1, bf16[256,768]{1,0:T(8,128)(2,1)} %w_qkv_hbm.1, ...), custom_call_target="tpu_custom_call" | custom-call | tf_op jit(solution)/shard_map/attend/pallas_call | solution.py:450
  15.3 0.0 copy-done
  15.3 0.0 copy-done.1
  15.3 0.0 copy-done.2
  15.3 5.1 %mlp.1 = bf16[2048,256]{1,0:T(8,128)(2,1)} custom-call(bf16[2048,256]{1,0:T(8,128)(2,1)S(1)} %get-tuple-element.8.mid, f32[32,256]{1,0:T(8,128)S(1)} %get-tuple-element.9.coarse, s32[1,2048]{1,0:T(1,128)S(1)} %copy-done.2, f32[1,256]{1,0:T(1,128)S(1)} %get-tuple-element.10.gain_mlp, bf16[256,1024]{1,0:T(8,128)(2,1)S(1)} %copy-done, ...), custom_call_target="tpu_custom_call" | custom-call | tf_op jit(solution)/shard_map/mlp/pallas_call | solution.py:504
Async XLA Ops:
  0.0 15.3 %copy-start = (bf16[256,1024]{1,0:T(8,128)(2,1)S(1)}, bf16[256,1024]{1,0:T(8,128)(2,1)}, u32[]{:S(2)}) copy-start(bf16[256,1024]{1,0:T(8,128)(2,1)} %w_up.1) | copy-start | bytes 1572868
  0.0 15.3 %copy-start.1 = (bf16[1024,256]{1,0:T(8,128)(2,1)S(1)}, bf16[1024,256]{1,0:T(8,128)(2,1)}, u32[]{:S(2)}) copy-start(bf16[1024,256]{1,0:T(8,128)(2,1)} %w_down.1) | copy-start | bytes 1572868
  0.0 15.3 %copy-start.2 = (s32[1,2048]{1,0:T(1,128)S(1)}, s32[1,2048]{1,0:T(1,128)}, u32[]{:S(2)}) copy-start(s32[1,2048]{1,0:T(1,128)} %order.1) | copy-start | bytes 24580

commit v4 on v3

--- a/solution.py
+++ b/solution.py
@@ -74,8 +74,8 @@
     c_out,
     points_sem,
     load_sem,
-    seq_send,
-    rep_send,
+    direct_send,
+    pair_send,
     recv_sem,
 ):
     seq_n, rep_n, heads = sizes
@@ -90,6 +90,9 @@
     my_seq = lax.axis_index("seq")
     my_rep = lax.axis_index("rep")
     me = my_seq * rep_n + my_rep
+    pair = 2 if rep_n % 2 == 0 else 1
+    pairs = rep_n // pair
+    direct = seq_n * pairs - 1
 
     small = [
         pltpu.make_async_copy(source, target, load_sem.at[n])
@@ -123,18 +126,35 @@
 
     barrier = pltpu.get_barrier_semaphore()
 
-    def greet_seq(step, carry):
-        place = {"seq": lax.rem(my_seq + step, seq_n), "rep": my_rep}
-        pl.semaphore_signal(barrier, inc=1, device_id=place, device_id_type=MESH)
-        return carry
-
-    def greet_rep(step, carry):
-        place = {"seq": my_seq, "rep": lax.rem(my_rep + step, rep_n)}
-        pl.semaphore_signal(barrier, inc=1, device_id=place, device_id_type=MESH)
-        return carry
-
-    lax.fori_loop(1, seq_n, greet_seq, 0)
-    lax.fori_loop(1, rep_n, greet_rep, 0)
+    def each(count, first, act):
+        def body(step, carry):
+            act(step)
+            return carry
+
+        lax.fori_loop(first, count, body, 0)
+
+    def seq_place(step):
+        above = seq_n - 1 - my_seq
+        rising = jnp.where(step < above, seq_n - 1 - step, step - above)
+        falling = jnp.where(step < my_seq, step, seq_n - 1 - step + my_seq)
+        return jnp.where(my_seq < seq_n // 2, rising, falling)
+
+    def place_of(step):
+        away = step // pairs
+        seq = jnp.where(away < seq_n - 1, seq_place(away), my_seq)
+        rep = lax.rem(my_rep + pair * (1 + lax.rem(step, pairs)), rep_n)
+        return seq, rep
+
+    def partner_of(step):
+        return my_rep - lax.rem(my_rep, pair) + lax.rem(my_rep + step, pair)
+
+    def greet(seq, rep):
+        pl.semaphore_signal(
+            barrier, inc=1, device_id={"seq": seq, "rep": rep}, device_id_type=MESH
+        )
+
+    each(direct, 0, lambda step: greet(*place_of(step)))
+    each(pair, 1, lambda step: greet(my_seq, partner_of(step)))
 
     small[0].wait()
     order_twice[...] = order[...] * 2
@@ -212,60 +232,38 @@
     own_block = stage[...].astype(BF)
     tokens_all[me] = own_block
 
-    pl.semaphore_wait(barrier, seq_n + rep_n - 2)
-
-    def seq_place(step):
-        low = my_seq < seq_n // 2
-        above = seq_n - 1 - my_seq
-        rising = jnp.where(step < above, seq_n - 1 - step, step - above)
-        falling = jnp.where(step < my_seq, step, seq_n - 1 - step + my_seq)
-        return jnp.where(low, rising, falling)
-
-    def seq_copy(step):
-        return pltpu.make_async_remote_copy(
-            src_ref=tokens_all.at[me],
-            dst_ref=tokens_all.at[me],
-            send_sem=seq_send.at[step],
-            recv_sem=recv_sem.at[me],
-            device_id={"seq": seq_place(step), "rep": my_rep},
-            device_id_type=MESH,
-        )
-
-    def rep_copy(block_seq, step):
-        block = block_seq * rep_n + my_rep
+    pl.semaphore_wait(barrier, direct + pair - 1)
+
+    def copy_of(block, send_sem, seq, rep):
         return pltpu.make_async_remote_copy(
             src_ref=tokens_all.at[block],
             dst_ref=tokens_all.at[block],
-            send_sem=rep_send.at[block_seq, step],
+            send_sem=send_sem,
             recv_sem=recv_sem.at[block],
-            device_id={"seq": my_seq, "rep": lax.rem(my_rep + step, rep_n)},
+            device_id={"seq": seq, "rep": rep},
             device_id_type=MESH,
         )
 
+    def spread(step):
+        return copy_of(me, direct_send.at[step], *place_of(step))
+
+    def forward(block, step):
+        return copy_of(block, pair_send.at[block, step], my_seq, partner_of(step))
+
     def arrival(block):
-        return pltpu.make_async_remote_copy(
-            src_ref=tokens_all.at[block],
-            dst_ref=tokens_all.at[block],
-            send_sem=seq_send.at[0],
-            recv_sem=recv_sem.at[block],
-            device_id={"seq": lax.rem(my_seq + 1, seq_n), "rep": my_rep},
-            device_id_type=MESH,
-        )
-
-    def each(count, first, act):
-        def body(step, carry):
-            act(step)
-            return carry
-
-        lax.fori_loop(first, count, body, 0)
-
-    each(seq_n - 1, 0, lambda step: seq_copy(step).start())
-    each(rep_n, 1, lambda step: rep_copy(my_seq, step).start())
+        return copy_of(block, direct_send.at[0], *place_of(0))
+
+    each(direct, 0, lambda step: spread(step).start())
+    each(pair, 1, lambda step: forward(me, step).start())
+
+    def block_of(step):
+        seq, rep = place_of(direct - 1 - step)
+        return seq * rep_n + rep
 
     def relay(step):
-        place = seq_place(seq_n - 2 - step)
-        arrival(place * rep_n + my_rep).wait_recv()
-        each(rep_n, 1, lambda away: rep_copy(place, away).start())
+        block = block_of(step)
+        arrival(block).wait_recv()
+        each(pair, 1, lambda away: forward(block, away).start())
 
     for load in loads:
         load.wait()
@@ -300,11 +298,11 @@
         return carry
 
     early = chunks // 2
-    first = (seq_n - 1) // 2
+    first = direct // 2
     lax.fori_loop(0, early, ball_step, 0)
     each(first, 0, relay)
     lax.fori_loop(early, chunks - 1, ball_step, 0)
-    each(seq_n - 1, first, relay)
+    each(direct, first, relay)
     lax.fori_loop(chunks - 1, chunks, ball_step, 0)
 
     own_tokens = jnp.where(own_block < NO_TOKEN / 2, own_block, 0.0).astype(BF)
@@ -313,13 +311,12 @@
     queries = [by_head(q_c[:, slab]) for slab in slabs]
 
     def gathered(step):
-        def one(away):
-            rep = lax.rem(my_rep + step, rep_n)
-            arrival(lax.rem(my_seq + away, seq_n) * rep_n + rep).wait_recv()
-
-        each(seq_n, 0, one)
-
-    each(rep_n, 1, gathered)
+        rep = partner_of(step)
+        each(pairs, 0, lambda away: each(seq_n, 0, lambda seq: arrival(
+            seq * rep_n + lax.rem(rep + pair * away, rep_n)
+        ).wait_recv()))
+
+    each(pair, 1, gathered)
 
     group = math.gcd(peers, 16)
 
@@ -355,8 +352,11 @@
     mix = jnp.concatenate(slab_mixes, axis=1)
     coarse[...] = dot(mix.astype(BF), c_out[...])
 
-    each(seq_n - 1, 0, lambda step: seq_copy(step).wait_send())
-    each(seq_n, 0, lambda away: each(rep_n, 1, lambda step: rep_copy(away, step).wait_send()))
+    each(direct, 0, lambda step: spread(step).wait_send())
+    each(pair, 1, lambda step: forward(me, step).wait_send())
+    each(direct, 0, lambda step: each(
+        pair, 1, lambda away: forward(block_of(step), away).wait_send()
+    ))
 
 
 def mlp_kernel(
@@ -476,8 +476,8 @@
             pltpu.VMEM(c_out.shape, BF),
             dma((chunks,)),
             dma((10,)),
-            dma((seq_n,)),
-            dma((seq_n, rep_n)),
+            dma((peers,)),
+            dma((peers, 2)),
             dma((peers,)),
         ],
         compiler_params=pltpu.CompilerParams(

time: 20.5 us -> 20.2 us (0.985)
  Pallas kernels: 20.3 us -> 20 us
    pallas_call x1, Pallas kernels: 15.2 us -> 15 us  [on_device(): pl.pallas_call(functools.partial(attend_kernel, (*sizes, heads)), out_sha...]
where the time goes in v4:
time: 20.2 us; the launch traced here: 20.1 us
  Pallas kernels  20 us (99%)
    pallas_call x1, Pallas kernels, on_device(): pl.pallas_call(functools.partial(attend_kernel, (*sizes, heads)), out_sha...  15 us
    pallas_call x1, Pallas kernels, on_device(): pl.pallas_call(mlp_kernel, out_shape=jax.ShapeDtypeStruct(points.shape, p...  5.09 us

profile of v4, /device:TPU:0, one launch (start us, length us, event | category | flops | bytes accessed | tf_op | source)
XLA Modules:
  0.0 20.1 jit_solution(13427929755218124252)
XLA Ops:
  0.0 0.0 copy-start
  0.0 0.0 copy-start.1
  0.0 0.0 copy-start.2
  0.0 15.0 %attend.1 = (bf16[2048,256]{1,0:T(8,128)(2,1)S(1)}, f32[32,256]{1,0:T(8,128)S(1)}, f32[1,256]{1,0:T(1,128)S(1)}) custom-call(bf16[2048,256]{1,0:T(8,128)(2,1)} %points_hbm.1, s32[1,2048]{1,0:T(1,128)} %order.1, s32[16]{0:T(128)} %counts_hbm.1, f32[1,256]{1,0:T(1,128)} %bitcast.2, f32[2,8]{1,0:T(2,128)} %temps_hbm.1, bf16[256,768]{1,0:T(8,128)(2,1)} %w_qkv_hbm.1, ...), custom_call_target="tpu_custom_call" | custom-call | tf_op jit(solution)/shard_map/attend/pallas_call | solution.py:450
  15.0 0.0 copy-done
  15.0 0.0 copy-done.1
  15.0 0.0 copy-done.2
  15.0 5.1 %mlp.1 = bf16[2048,256]{1,0:T(8,128)(2,1)} custom-call(bf16[2048,256]{1,0:T(8,128)(2,1)S(1)} %get-tuple-element.8.mid, f32[32,256]{1,0:T(8,128)S(1)} %get-tuple-element.9.coarse, s32[1,2048]{1,0:T(1,128)S(1)} %copy-done.2, f32[1,256]{1,0:T(1,128)S(1)} %get-tuple-element.10.gain_mlp, bf16[256,1024]{1,0:T(8,128)(2,1)S(1)} %copy-done, ...), custom_call_target="tpu_custom_call" | custom-call | tf_op jit(solution)/shard_map/mlp/pallas_call | solution.py:504
Async XLA Ops:
  0.0 15.0 %copy-start = (bf16[256,1024]{1,0:T(8,128)(2,1)S(1)}, bf16[256,1024]{1,0:T(8,128)(2,1)}, u32[]{:S(2)}) copy-start(bf16[256,1024]{1,0:T(8,128)(2,1)} %w_up.1) | copy-start | bytes 1572868
  0.0 15.0 %copy-start.1 = (bf16[1024,256]{1,0:T(8,128)(2,1)S(1)}, bf16[1024,256]{1,0:T(8,128)(2,1)}, u32[]{:S(2)}) copy-start(bf16[1024,256]{1,0:T(8,128)(2,1)} %w_down.1) | copy-start | bytes 1572868
  0.0 15.0 %copy-start.2 = (s32[1,2048]{1,0:T(1,128)S(1)}, s32[1,2048]{1,0:T(1,128)}, u32[]{:S(2)}) copy-start(s32[1,2048]{1,0:T(1,128)} %order.1) | copy-start | bytes 24580

commit v5 on v4

--- a/solution.py
+++ b/solution.py
@@ -66,6 +66,9 @@
     picked,
     srt,
     nrm,
+    queries,
+    keys,
+    values,
     stage,
     tokens_all,
     w_qkv,
@@ -193,8 +196,10 @@
     for load in small[1:]:
         load.wait()
     load_spots.wait()
+    loads[0].wait()
 
     gain_a = gain_attn[...]
+    q_scale = lane_scale(0)
 
     def gather_chunk(i):
         for r in range(i * chunk, (i + 1) * chunk):
@@ -223,6 +228,13 @@
             half_f > 0.0, total / jnp.maximum(half_f, 1.0), NO_TOKEN
         )
 
+    def qkv_chunk(i):
+        spot = pl.ds(i * chunk, chunk)
+        joined = dot(nrm[spot, :], w_qkv[...])
+        queries[spot, :] = (head_rms(joined[:, :width]) * q_scale).astype(BF)
+        keys[spot, :] = head_rms(joined[:, width : 2 * width]).astype(BF)
+        values[spot, :] = joined[:, 2 * width :].astype(BF)
+
     gather_chunk(0)
     for i in range(1, chunks):
         gather_chunk(i)
@@ -265,50 +277,45 @@
         arrival(block).wait_recv()
         each(pair, 1, lambda away: forward(block, away).start())
 
-    for load in loads:
+    for load in loads[1:]:
         load.wait()
 
-    q_scale = lane_scale(0)
-
-    def ball_chunk(i, carry):
-        base = pl.multiple_of(i * chunk, chunk)
-        spot = pl.ds(base, chunk)
-        joined = dot(nrm[spot, :], w_qkv[...])
-        q = (head_rms(joined[:, :width]) * q_scale).astype(BF)
-        k = head_rms(joined[:, width : 2 * width]).astype(BF)
-        v = joined[:, 2 * width :]
+    def ball_chunk(i):
         mixes = []
         for b in range(4):
-            part = slice(b * BALL, (b + 1) * BALL)
-            live = lax.broadcasted_iota(jnp.int32, (BALL, width), 0) < counts[i * 4 + b]
-            vb = jnp.where(live, v[part], 0.0).astype(BF)
-            ones = by_head(jnp.where(live[:, :LANES], 1.0, 0.0).astype(BF))
+            spot = pl.ds(i * chunk + b * BALL, BALL)
+            q, k, v = queries[spot, :], keys[spot, :], values[spot, :]
+            live = lax.broadcasted_iota(jnp.int32, (BALL, LANES), 0) < counts[i * 4 + b]
+            there = jnp.where(live, 1.0, 0.0).astype(BF)
+            alive = [there * lanes for lanes in head_lanes]
+            ones = jnp.concatenate(alive, axis=0)
             slab_mixes = []
             for slab in slabs:
-                weights = jnp.exp2(dot_t(q[part, slab], by_head(k[part, slab]))).astype(BF)
-                mixed = dot(weights, jnp.concatenate([by_head(vb[:, slab]), ones], axis=1))
+                weights = jnp.exp2(dot_t(q[:, slab], by_head(k[:, slab]))).astype(BF)
+                seen = jnp.concatenate([v[:, slab] * lanes for lanes in alive], axis=0)
+                mixed = dot(weights, jnp.concatenate([seen, ones], axis=1))
                 slab_mixes.append((mixed[:, :LANES] / mixed[:, LANES:]).astype(BF))
             mixes.append(jnp.concatenate(slab_mixes, axis=1))
         fine = dot(jnp.concatenate(mixes, axis=0), w_out[...])
+        spot = pl.ds(i * chunk, chunk)
         mid[spot, :] = (srt[spot, :].astype(F32) + fine).astype(BF)
-        return carry
-
-    def ball_step(i, carry):
-        ball_chunk(i, carry)
-        return carry
 
     early = chunks // 2
     first = direct // 2
-    lax.fori_loop(0, early, ball_step, 0)
-    each(first, 0, relay)
-    lax.fori_loop(early, chunks - 1, ball_step, 0)
-    each(direct, first, relay)
-    lax.fori_loop(chunks - 1, chunks, ball_step, 0)
+    qkv_chunk(0)
+    for i in range(chunks):
+        if i + 1 < chunks:
+            qkv_chunk(i + 1)
+        ball_chunk(i)
+        if i == early - 1:
+            each(first, 0, relay)
+        if i == chunks - 2:
+            each(direct, first, relay)
 
     own_tokens = jnp.where(own_block < NO_TOKEN / 2, own_block, 0.0).astype(BF)
     q_c = dot(own_tokens, c_qkv[:, :width])
     q_c = (head_rms(q_c) * lane_scale(1)).astype(BF)
-    queries = [by_head(q_c[:, slab]) for slab in slabs]
+    coarse_queries = [by_head(q_c[:, slab]) for slab in slabs]
 
     def gathered(step):
         rep = partner_of(step)
@@ -325,12 +332,12 @@
         there = block < NO_TOKEN / 2
         ones = jnp.where(there[:, :LANES], 1.0, 0.0).astype(BF)
         joined = dot(jnp.where(there, block, 0.0).astype(BF), c_qkv[:, width:])
-        keys = head_rms(joined[:, :width]).astype(BF)
-        values = joined[:, width:].astype(BF)
+        c_keys = head_rms(joined[:, :width]).astype(BF)
+        c_values = joined[:, width:].astype(BF)
         sums = []
-        for query, slab in zip(queries, slabs):
-            weights = jnp.exp2(dot_t(query, keys[:, slab])).astype(BF)
-            sums.append(dot(weights, jnp.concatenate([values[:, slab], ones], axis=1)))
+        for query, slab in zip(coarse_queries, slabs):
+            weights = jnp.exp2(dot_t(query, c_keys[:, slab])).astype(BF)
+            sums.append(dot(weights, jnp.concatenate([c_values[:, slab], ones], axis=1)))
         return sums
 
     if peers == group:
@@ -468,6 +475,9 @@
             pltpu.VMEM((tall, LANES), F32),
             pltpu.VMEM((rows, width), BF),
             pltpu.VMEM((rows, width), BF),
+            pltpu.VMEM((rows, width), BF),
+            pltpu.VMEM((rows, width), BF),
+            pltpu.VMEM((rows, width), BF),
             pltpu.VMEM((coarse_rows, width), F32),
             pltpu.VMEM((peers, coarse_rows, width), BF),
             pltpu.VMEM(w_qkv.shape, BF),

time: 20.2 us -> 19.8 us (0.980)
  Pallas kernels: 20 us -> 19.6 us
    pallas_call x1, Pallas kernels: 15 us -> 14.5 us  [on_device(): pl.pallas_call(functools.partial(attend_kernel, (*sizes, heads)), out_sha...]
where the time goes in v5:
time: 19.8 us; the launch traced here: 19.7 us
  Pallas kernels  19.6 us (99%)
    pallas_call x1, Pallas kernels, on_device(): pl.pallas_call(functools.partial(attend_kernel, (*sizes, heads)), out_sha...  14.5 us
    pallas_call x1, Pallas kernels, on_device(): pl.pallas_call(mlp_kernel, out_shape=jax.ShapeDtypeStruct(points.shape, p...  5.09 us

profile of v5, /device:TPU:0, one launch (start us, length us, event | category | flops | bytes accessed | tf_op | source)
XLA Modules:
  0.0 19.7 jit_solution(18324452483612191056)
XLA Ops:
  0.0 0.0 copy-start
  0.0 0.0 copy-start.1
  0.0 0.0 copy-start.2
  0.0 14.5 %attend.1 = (bf16[2048,256]{1,0:T(8,128)(2,1)S(1)}, f32[32,256]{1,0:T(8,128)S(1)}, f32[1,256]{1,0:T(1,128)S(1)}) custom-call(bf16[2048,256]{1,0:T(8,128)(2,1)} %points_hbm.1, s32[1,2048]{1,0:T(1,128)} %order.1, s32[16]{0:T(128)} %counts_hbm.1, f32[1,256]{1,0:T(1,128)} %bitcast.2, f32[2,8]{1,0:T(2,128)} %temps_hbm.1, bf16[256,768]{1,0:T(8,128)(2,1)} %w_qkv_hbm.1, ...), custom_call_target="tpu_custom_call" | custom-call | tf_op jit(solution)/shard_map/attend/pallas_call | solution.py:457
  14.5 0.0 copy-done
  14.6 0.0 copy-done.1
  14.6 0.0 copy-done.2
  14.6 5.1 %mlp.1 = bf16[2048,256]{1,0:T(8,128)(2,1)} custom-call(bf16[2048,256]{1,0:T(8,128)(2,1)S(1)} %get-tuple-element.8.mid, f32[32,256]{1,0:T(8,128)S(1)} %get-tuple-element.9.coarse, s32[1,2048]{1,0:T(1,128)S(1)} %copy-done.2, f32[1,256]{1,0:T(1,128)S(1)} %get-tuple-element.10.gain_mlp, bf16[256,1024]{1,0:T(8,128)(2,1)S(1)} %copy-done, ...), custom_call_target="tpu_custom_call" | custom-call | tf_op jit(solution)/shard_map/mlp/pallas_call | solution.py:514
Async XLA Ops:
  0.0 14.5 %copy-start = (bf16[256,1024]{1,0:T(8,128)(2,1)S(1)}, bf16[256,1024]{1,0:T(8,128)(2,1)}, u32[]{:S(2)}) copy-start(bf16[256,1024]{1,0:T(8,128)(2,1)} %w_up.1) | copy-start | bytes 1572868
  0.0 14.6 %copy-start.1 = (bf16[1024,256]{1,0:T(8,128)(2,1)S(1)}, bf16[1024,256]{1,0:T(8,128)(2,1)}, u32[]{:S(2)}) copy-start(bf16[1024,256]{1,0:T(8,128)(2,1)} %w_down.1) | copy-start | bytes 1572868
  0.0 14.6 %copy-start.2 = (s32[1,2048]{1,0:T(1,128)S(1)}, s32[1,2048]{1,0:T(1,128)}, u32[]{:S(2)}) copy-start(s32[1,2048]{1,0:T(1,128)} %order.1) | copy-start | bytes 24580

commit v6 on v5

--- a/solution.py
+++ b/solution.py
@@ -300,17 +300,15 @@
         spot = pl.ds(i * chunk, chunk)
         mid[spot, :] = (srt[spot, :].astype(F32) + fine).astype(BF)
 
-    early = chunks // 2
     first = direct // 2
     qkv_chunk(0)
     for i in range(chunks):
         if i + 1 < chunks:
             qkv_chunk(i + 1)
         ball_chunk(i)
-        if i == early - 1:
+        if i == chunks - 2:
             each(first, 0, relay)
-        if i == chunks - 2:
-            each(direct, first, relay)
+    each(direct, first, relay)
 
     own_tokens = jnp.where(own_block < NO_TOKEN / 2, own_block, 0.0).astype(BF)
     q_c = dot(own_tokens, c_qkv[:, :width])
@@ -323,12 +321,15 @@
             seq * rep_n + lax.rem(rep + pair * away, rep_n)
         ).wait_recv()))
 
-    each(pair, 1, gathered)
-
-    group = math.gcd(peers, 16)
-
-    def coarse_keys(g):
-        block = tokens_all[pl.ds(g * group, group)].reshape(group * coarse_rows, width)
+    blocks = seq_n * pairs
+    group = math.gcd(blocks, 8)
+
+    def coarse_keys(side, g):
+        members = [
+            (g * group + t) // pairs * rep_n + (g * group + t) % pairs * pair + side
+            for t in range(group)
+        ]
+        block = jnp.concatenate([tokens_all[member] for member in members], axis=0)
         there = block < NO_TOKEN / 2
         ones = jnp.where(there[:, :LANES], 1.0, 0.0).astype(BF)
         joined = dot(jnp.where(there, block, 0.0).astype(BF), c_qkv[:, width:])
@@ -340,15 +341,20 @@
             sums.append(dot(weights, jnp.concatenate([c_values[:, slab], ones], axis=1)))
         return sums
 
-    if peers == group:
-        sums = coarse_keys(0)
-    else:
-        sums = lax.fori_loop(
+    def coarse_side(side):
+        if blocks == group:
+            return coarse_keys(side, 0)
+        return lax.fori_loop(
             0,
-            peers // group,
-            lambda g, total: [a + b for a, b in zip(total, coarse_keys(g))],
+            blocks // group,
+            lambda g, total: [a + b for a, b in zip(total, coarse_keys(side, g))],
             [jnp.zeros((near_heads * coarse_rows, 2 * LANES), F32) for _ in slabs],
         )
+
+    sums = coarse_side(lax.rem(my_rep, pair))
+    each(pair, 1, gathered)
+    if pair > 1:
+        sums = [a + b for a, b in zip(sums, coarse_side(lax.rem(my_rep + 1, pair)))]
     slab_mixes = []
     for total in sums:
         ratio = total[:, :LANES] / total[:, LANES:]

time: 19.8 us -> 19.4 us (0.980)
  Pallas kernels: 19.6 us -> 19.2 us
    pallas_call x1, Pallas kernels: 14.5 us -> 14.1 us  [on_device(): pl.pallas_call(functools.partial(attend_kernel, (*sizes, heads)), out_sha...]
where the time goes in v6:
time: 19.4 us; the launch traced here: 19.2 us
  Pallas kernels  19.2 us (99%)
    pallas_call x1, Pallas kernels, on_device(): pl.pallas_call(functools.partial(attend_kernel, (*sizes, heads)), out_sha...  14.1 us
    pallas_call x1, Pallas kernels, on_device(): pl.pallas_call(mlp_kernel, out_shape=jax.ShapeDtypeStruct(points.shape, p...  5.09 us

profile of v6, /device:TPU:0, one launch (start us, length us, event | category | flops | bytes accessed | tf_op | source)
XLA Modules:
  0.0 19.2 jit_solution(13546908151372026622)
XLA Ops:
  0.0 0.0 copy-start
  0.0 0.0 copy-start.1
  0.0 0.0 copy-start.2
  0.0 14.1 %attend.1 = (bf16[2048,256]{1,0:T(8,128)(2,1)S(1)}, f32[32,256]{1,0:T(8,128)S(1)}, f32[1,256]{1,0:T(1,128)S(1)}) custom-call(bf16[2048,256]{1,0:T(8,128)(2,1)} %points_hbm.1, s32[1,2048]{1,0:T(1,128)} %order.1, s32[16]{0:T(128)} %counts_hbm.1, f32[1,256]{1,0:T(1,128)} %bitcast.2, f32[2,8]{1,0:T(2,128)} %temps_hbm.1, bf16[256,768]{1,0:T(8,128)(2,1)} %w_qkv_hbm.1, ...), custom_call_target="tpu_custom_call" | custom-call | tf_op jit(solution)/shard_map/attend/pallas_call | solution.py:463
  14.1 0.0 copy-done
  14.1 0.0 copy-done.1
  14.1 0.0 copy-done.2
  14.1 5.1 %mlp.1 = bf16[2048,256]{1,0:T(8,128)(2,1)} custom-call(bf16[2048,256]{1,0:T(8,128)(2,1)S(1)} %get-tuple-element.8.mid, f32[32,256]{1,0:T(8,128)S(1)} %get-tuple-element.9.coarse, s32[1,2048]{1,0:T(1,128)S(1)} %copy-done.2, f32[1,256]{1,0:T(1,128)S(1)} %get-tuple-element.10.gain_mlp, bf16[256,1024]{1,0:T(8,128)(2,1)S(1)} %copy-done, ...), custom_call_target="tpu_custom_call" | custom-call | tf_op jit(solution)/shard_map/mlp/pallas_call | solution.py:520
Async XLA Ops:
  0.0 14.1 %copy-start = (bf16[256,1024]{1,0:T(8,128)(2,1)S(1)}, bf16[256,1024]{1,0:T(8,128)(2,1)}, u32[]{:S(2)}) copy-start(bf16[256,1024]{1,0:T(8,128)(2,1)} %w_up.1) | copy-start | bytes 1572868
  0.0 14.1 %copy-start.1 = (bf16[1024,256]{1,0:T(8,128)(2,1)S(1)}, bf16[1024,256]{1,0:T(8,128)(2,1)}, u32[]{:S(2)}) copy-start(bf16[1024,256]{1,0:T(8,128)(2,1)} %w_down.1) | copy-start | bytes 1572868
  0.0 14.1 %copy-start.2 = (s32[1,2048]{1,0:T(1,128)S(1)}, s32[1,2048]{1,0:T(1,128)}, u32[]{:S(2)}) copy-start(s32[1,2048]{1,0:T(1,128)} %order.1) | copy-start | bytes 24580

commit v7 on v6

--- a/solution.py
+++ b/solution.py
@@ -17,6 +17,7 @@
 GELU_A = math.sqrt(2.0 / math.pi)
 GELU_B = 0.044715 * math.sqrt(2.0 / math.pi)
 NO_TOKEN = 1024.0
+GELU_SCALE = (8.0 * GELU_B) ** (1.0 / 3.0)
 LOG2E = 1.4426950408889634
 MESH = pl.DeviceIdType.MESH
 BF = jnp.bfloat16
@@ -31,9 +32,8 @@
     return lax.dot_general(a, b, (((1,), (1,)), ((), ())), preferred_element_type=F32)
 
 
-def gelu_of_half(half):
-    inner = half * (2.0 * GELU_A + 8.0 * GELU_B * (half * half))
-    return half + half * jnp.tanh(inner)
+def scaled_gelu(scaled):
+    return scaled + scaled * jnp.tanh(scaled * (2.0 * GELU_A / GELU_SCALE + scaled * scaled))
 
 
 def rms(values, gain):
@@ -52,11 +52,16 @@
     c_qkv_hbm,
     c_out_hbm,
     gain_mlp_hbm,
+    w_up_hbm,
+    w_down_hbm,
     mid,
     coarse,
     gain_mid,
+    upward,
+    w_up,
+    w_down,
+    order,
     points,
-    order,
     order_twice,
     gain_attn,
     spots,
@@ -112,10 +117,12 @@
                 (c_qkv_hbm, c_qkv),
                 (c_out_hbm, c_out),
                 (gain_mlp_hbm, gain_mid),
+                (w_up_hbm, w_up),
+                (w_down_hbm, w_down),
             ]
         )
     ]
-    load_spots = pltpu.make_async_copy(order_twice, spots, load_sem.at[9])
+    load_spots = pltpu.make_async_copy(order_twice, spots, load_sem.at[11])
 
     def enter(i):
         spot = pl.ds(i * chunk, chunk)
@@ -298,7 +305,9 @@
             mixes.append(jnp.concatenate(slab_mixes, axis=1))
         fine = dot(jnp.concatenate(mixes, axis=0), w_out[...])
         spot = pl.ds(i * chunk, chunk)
-        mid[spot, :] = (srt[spot, :].astype(F32) + fine).astype(BF)
+        near_mid = srt[spot, :].astype(F32) + fine
+        mid[spot, :] = near_mid.astype(BF)
+        upward[spot, :] = dot((near_mid * (gain_mid[...] * (0.5 * GELU_SCALE))).astype(BF), w_up[...]).astype(BF)
 
     first = direct // 2
     qkv_chunk(0)
@@ -375,11 +384,13 @@
 def mlp_kernel(
     mid,
     coarse,
-    order,
     gain_mlp,
+    upward,
     w_up,
     w_down,
+    order,
     out,
+    coarse_up,
     res,
     ready,
     packed,
@@ -392,11 +403,12 @@
     chunk = 4 * BALL
     chunks = rows // chunk
     tokens = chunk // POOL
-    gain_half = gain_mlp[...] * 0.5
+    ffn = upward.shape[1]
 
     order_twice[...] = order[...] * 2
     load_spots = pltpu.make_async_copy(order_twice, spots, load_sem)
     load_spots.start()
+    coarse_up[...] = dot((coarse[...] * (gain_mlp[...] * (0.5 * GELU_SCALE))).astype(BF), w_up[...])
 
     def mlp_chunk(i):
         terms = coarse[pl.ds(i * tokens, tokens), :]
@@ -404,9 +416,20 @@
             [jnp.broadcast_to(terms[t : t + 1], (POOL, width)) for t in range(tokens)], axis=0
         )
         middle = mid[pl.ds(i * chunk, chunk), :].astype(F32) + spread
-        mlp_in = rms(middle, gain_half).astype(BF)
-        activated = gelu_of_half(dot(mlp_in, w_up[...]).astype(BF))
-        result = middle + dot(activated, w_down[...])
+        scale = lax.rsqrt(jnp.mean(middle * middle, axis=-1, keepdims=True) + EPS)
+        scale = jnp.broadcast_to(scale, (chunk, LANES)).astype(BF)
+        lifts = []
+        for t in range(tokens):
+            lift = coarse_up[pl.ds(i * tokens + t, 1), :]
+            lifts += [jnp.broadcast_to(lift, (16, ffn)).astype(BF)] * (POOL // 16)
+        half = upward[pl.ds(i * chunk, chunk), :] + jnp.concatenate(lifts, axis=0)
+        half = half * jnp.concatenate([scale] * (ffn // LANES), axis=1)
+        activated = scaled_gelu(half)
+        down = jnp.concatenate(
+            [dot(activated[: chunk // 2], w_down[...]), dot(activated[chunk // 2 :], w_down[...])],
+            axis=0,
+        )
+        result = middle + down * (1.0 / GELU_SCALE)
         for n in range(width // LANES):
             res[pl.ds(2 * i * chunk + n, chunk, stride=2), :] = result[:, n * LANES : (n + 1) * LANES]
 
@@ -460,18 +483,21 @@
     far = pl.BlockSpec(memory_space=pl.ANY)
     dma = pltpu.SemaphoreType.DMA
     tall = rows * width // LANES
-    mid, coarse, gain_mid = pl.pallas_call(
+    mid, coarse, *rest = pl.pallas_call(
         functools.partial(attend_kernel, (*sizes, heads)),
         out_shape=(
             jax.ShapeDtypeStruct((rows, width), BF),
             jax.ShapeDtypeStruct((coarse_rows, width), F32),
             jax.ShapeDtypeStruct((1, width), F32),
+            jax.ShapeDtypeStruct((rows, w_up.shape[1]), BF),
+            jax.ShapeDtypeStruct(w_up.shape, BF),
+            jax.ShapeDtypeStruct(w_down.shape, BF),
+            jax.ShapeDtypeStruct((1, rows), jnp.int32),
         ),
-        in_specs=[hbm] * 10,
-        out_specs=(vmem,) * 3,
+        in_specs=[hbm] * 12,
+        out_specs=(vmem,) * 7,
         scratch_shapes=[
             pltpu.VMEM((rows, width), BF),
-            pltpu.VMEM((1, rows), jnp.int32),
             pltpu.VMEM((1, rows), jnp.int32),
             pltpu.VMEM((1, width), F32),
             pltpu.SMEM((1, rows), jnp.int32),
@@ -491,7 +517,7 @@
             pltpu.VMEM(c_qkv.shape, BF),
             pltpu.VMEM(c_out.shape, BF),
             dma((chunks,)),
-            dma((10,)),
+            dma((12,)),
             dma((peers,)),
             dma((peers, 2)),
             dma((peers,)),
@@ -514,15 +540,18 @@
                 c_qkv,
                 c_out,
                 gain_mlp.reshape(1, width),
+                w_up,
+                w_down,
             )
         )
     )
     return pl.pallas_call(
         mlp_kernel,
         out_shape=jax.ShapeDtypeStruct(points.shape, points.dtype),
-        in_specs=[vmem] * 6,
+        in_specs=[vmem] * 7,
         out_specs=far,
         scratch_shapes=[
+            pltpu.VMEM((coarse_rows, w_up.shape[1]), F32),
             pltpu.VMEM((tall, LANES), F32),
             pltpu.VMEM((tall, LANES), F32),
             pltpu.VMEM((rows, width), BF),
@@ -533,7 +562,7 @@
         ],
         compiler_params=pltpu.CompilerParams(vmem_limit_bytes=VMEM_MLP),
         name="mlp",
-    )(mid, coarse, ball_order, gain_mid, w_up, w_down)
+    )(mid, coarse, *rest)
 
 
 def solution(mesh):

time: 19.4 us -> 20.2 us (1.041)
  Pallas kernels: 19.2 us -> 19.8 us
    pallas_call x1, Pallas kernels: 14.1 us -> 15 us  [on_device(): pl.pallas_call(functools.partial(attend_kernel, (*sizes, heads)), out_sha...]
    pallas_call x1, Pallas kernels: 5.09 us -> 4.88 us  [on_device(): pl.pallas_call(mlp_kernel, out_shape=jax.ShapeDtypeStruct(points.shape, p...]
where the time goes in v7:
time: 20.2 us; the launch traced here: 20 us
  Pallas kernels  19.8 us (98%)
    pallas_call x1, Pallas kernels, on_device(): pl.pallas_call(functools.partial(attend_kernel, (*sizes, heads)), out_sha...  15 us
    pallas_call x1, Pallas kernels, on_device(): pl.pallas_call(mlp_kernel, out_shape=jax.ShapeDtypeStruct(points.shape, p...  4.88 us

profile of v7, /device:TPU:0, one launch (start us, length us, event | category | flops | bytes accessed | tf_op | source)
XLA Modules:
  0.0 20.0 jit_solution(12563182995767942725)
XLA Ops:
  0.0 15.0 %attend.1 = (bf16[2048,256]{1,0:T(8,128)(2,1)S(1)}, f32[32,256]{1,0:T(8,128)S(1)}, f32[1,256]{1,0:T(1,128)S(1)}, bf16[2048,1024]{1,0:T(8,128)(2,1)S(1)}, bf16[25...) custom-call(bf16[2048,256]{1,0:T(8,128)(2,1)} %points_hbm.1, s32[1,2048]{1,0:T(1,128)} %order_hbm.1, ...), custom_call_target="tpu_custom_call" | custom-call | tf_op jit(solution)/shard_map/attend/pallas_call | solution.py:486
  15.0 4.9 %mlp.1 = bf16[2048,256]{1,0:T(8,128)(2,1)} custom-call(bf16[2048,256]{1,0:T(8,128)(2,1)S(1)} %get-tuple-element.12.mid, f32[32,256]{1,0:T(8,128)S(1)} %get-tuple-element.13.coarse, f32[1,256]{1,0:T(1,128)S(1)} %get-tuple-element.14.gain_mlp, bf16[2048,1024]{1,0:T(8,128)(2,1)S(1)} %get-tuple-element.15.upward, bf16[256,1024]{1,0:T(8,128)(2,1)S(1)} %get-tuple-element.16.w_up, ...), custom_call_target="tpu_custom_call" | custom-call | tf_op jit(solution)/shard_map/mlp/pallas_call | solution.py:548

commit v8 on v6

--- a/solution.py
+++ b/solution.py
@@ -96,6 +96,9 @@
     pair = 2 if rep_n % 2 == 0 else 1
     pairs = rep_n // pair
     direct = seq_n * pairs - 1
+    parts = 2 if chunks % 2 == 0 and chunks > 2 else 1
+    part_chunks = chunks // parts
+    part_rows = coarse_rows // parts
 
     small = [
         pltpu.make_async_copy(source, target, load_sem.at[n])
@@ -201,8 +204,8 @@
     gain_a = gain_attn[...]
     q_scale = lane_scale(0)
 
-    def gather_chunk(i):
-        for r in range(i * chunk, (i + 1) * chunk):
+    def gather_rows(first_row, count):
+        for r in range(first_row, first_row + count):
             picked[pl.ds(2 * r, 2), :] = wide[pl.ds(spots[0, r], 2), :]
 
     def pool_chunk(i):
@@ -235,38 +238,33 @@
         keys[spot, :] = head_rms(joined[:, width : 2 * width]).astype(BF)
         values[spot, :] = joined[:, 2 * width :].astype(BF)
 
-    gather_chunk(0)
-    for i in range(1, chunks):
-        gather_chunk(i)
-        pool_chunk(i - 1)
-    pool_chunk(chunks - 1)
-
-    own_block = stage[...].astype(BF)
-    tokens_all[me] = own_block
-
-    pl.semaphore_wait(barrier, direct + pair - 1)
-
-    def copy_of(block, send_sem, seq, rep):
+    def copy_of(block, part, send_sem, seq, rep):
+        share = pl.ds(part * part_rows, part_rows)
         return pltpu.make_async_remote_copy(
-            src_ref=tokens_all.at[block],
-            dst_ref=tokens_all.at[block],
+            src_ref=tokens_all.at[block, share],
+            dst_ref=tokens_all.at[block, share],
             send_sem=send_sem,
-            recv_sem=recv_sem.at[block],
+            recv_sem=recv_sem.at[part, block],
             device_id={"seq": seq, "rep": rep},
             device_id_type=MESH,
         )
 
-    def spread(step):
-        return copy_of(me, direct_send.at[step], *place_of(step))
-
-    def forward(block, step):
-        return copy_of(block, pair_send.at[block, step], my_seq, partner_of(step))
-
-    def arrival(block):
-        return copy_of(block, direct_send.at[0], *place_of(0))
-
-    each(direct, 0, lambda step: spread(step).start())
-    each(pair, 1, lambda step: forward(me, step).start())
+    def spread(part, step):
+        return copy_of(me, part, direct_send.at[part, step], *place_of(step))
+
+    def forward(part, block, step):
+        return copy_of(block, part, pair_send.at[part, block, step], my_seq, partner_of(step))
+
+    def arrival(part, block):
+        return copy_of(block, part, direct_send.at[part, 0], *place_of(0))
+
+    def publish(part):
+        share = pl.ds(part * part_rows, part_rows)
+        tokens_all[me, share] = stage[share, :].astype(BF)
+        if part == 0:
+            pl.semaphore_wait(barrier, direct + pair - 1)
+        each(direct, 0, lambda step: spread(part, step).start())
+        each(pair, 1, lambda step: forward(part, me, step).start())
 
     def block_of(step):
         seq, rep = place_of(direct - 1 - step)
@@ -274,8 +272,23 @@
 
     def relay(step):
         block = block_of(step)
-        arrival(block).wait_recv()
-        each(pair, 1, lambda away: forward(block, away).start())
+        for part in range(parts):
+            arrival(part, block).wait_recv()
+            each(pair, 1, lambda away: forward(part, block, away).start())
+
+    gather_rows(0, chunk)
+    for i in range(1, chunks):
+        early = part_chunks == i - 1
+        if early:
+            publish(0)
+        last = part_chunks == i + 0 and parts > 1
+        gather_rows(i * chunk + (chunk // 2 if early else 0), chunk // 2 if early else chunk)
+        pool_chunk(i - 1)
+        if last:
+            gather_rows((i + 1) * chunk, chunk // 2)
+    pool_chunk(chunks - 1)
+    publish(parts - 1)
+    own_block = stage[...].astype(BF)
 
     for load in loads[1:]:
         load.wait()
@@ -315,10 +328,10 @@
     q_c = (head_rms(q_c) * lane_scale(1)).astype(BF)
     coarse_queries = [by_head(q_c[:, slab]) for slab in slabs]
 
-    def gathered(step):
+    def gathered(part, step):
         rep = partner_of(step)
         each(pairs, 0, lambda away: each(seq_n, 0, lambda seq: arrival(
-            seq * rep_n + lax.rem(rep + pair * away, rep_n)
+            part, seq * rep_n + lax.rem(rep + pair * away, rep_n)
         ).wait_recv()))
 
     blocks = seq_n * pairs
@@ -352,7 +365,8 @@
         )
 
     sums = coarse_side(lax.rem(my_rep, pair))
-    each(pair, 1, gathered)
+    for part in range(parts):
+        each(pair, 1, functools.partial(gathered, part))
     if pair > 1:
         sums = [a + b for a, b in zip(sums, coarse_side(lax.rem(my_rep + 1, pair)))]
     slab_mixes = []
@@ -365,11 +379,12 @@
     mix = jnp.concatenate(slab_mixes, axis=1)
     coarse[...] = dot(mix.astype(BF), c_out[...])
 
-    each(direct, 0, lambda step: spread(step).wait_send())
-    each(pair, 1, lambda step: forward(me, step).wait_send())
-    each(direct, 0, lambda step: each(
-        pair, 1, lambda away: forward(block_of(step), away).wait_send()
-    ))
+    for part in range(parts):
+        each(direct, 0, lambda step: spread(part, step).wait_send())
+        each(pair, 1, lambda step: forward(part, me, step).wait_send())
+        each(direct, 0, lambda step: each(
+            pair, 1, lambda away: forward(part, block_of(step), away).wait_send()
+        ))
 
 
 def mlp_kernel(
@@ -492,9 +507,9 @@
             pltpu.VMEM(c_out.shape, BF),
             dma((chunks,)),
             dma((10,)),
-            dma((peers,)),
-            dma((peers, 2)),
-            dma((peers,)),
+            dma((2, peers)),
+            dma((2, peers, 2)),
+            dma((2, peers)),
         ],
         compiler_params=pltpu.CompilerParams(
             collective_id=0, has_side_effects=True, vmem_limit_bytes=VMEM_ATTEND

time: 19.4 us -> 20.4 us (1.052)
  Pallas kernels: 19.2 us -> 20.2 us
    pallas_call x1, Pallas kernels: 14.1 us -> 15.1 us  [on_device(): pl.pallas_call(functools.partial(attend_kernel, (*sizes, heads)), out_sha...]
where the time goes in v8:
time: 20.4 us; the launch traced here: 20.3 us
  Pallas kernels  20.2 us (99%)
    pallas_call x1, Pallas kernels, on_device(): pl.pallas_call(functools.partial(attend_kernel, (*sizes, heads)), out_sha...  15.1 us
    pallas_call x1, Pallas kernels, on_device(): pl.pallas_call(mlp_kernel, out_shape=jax.ShapeDtypeStruct(points.shape, p...  5.09 us

profile of v8, /device:TPU:0, one launch (start us, length us, event | category | flops | bytes accessed | tf_op | source)
XLA Modules:
  0.0 20.3 jit_solution(10346620091019656894)
XLA Ops:
  0.0 0.0 copy-start
  0.0 0.0 copy-start.1
  0.0 0.0 copy-start.2
  0.0 15.1 %attend.1 = (bf16[2048,256]{1,0:T(8,128)(2,1)S(1)}, f32[32,256]{1,0:T(8,128)S(1)}, f32[1,256]{1,0:T(1,128)S(1)}) custom-call(bf16[2048,256]{1,0:T(8,128)(2,1)} %points_hbm.1, s32[1,2048]{1,0:T(1,128)} %order.1, s32[16]{0:T(128)} %counts_hbm.1, f32[1,256]{1,0:T(1,128)} %bitcast.2, f32[2,8]{1,0:T(2,128)} %temps_hbm.1, bf16[256,768]{1,0:T(8,128)(2,1)} %w_qkv_hbm.1, ...), custom_call_target="tpu_custom_call" | custom-call | tf_op jit(solution)/shard_map/attend/pallas_call | solution.py:478
  15.2 0.0 copy-done
  15.2 0.0 copy-done.1
  15.2 0.0 copy-done.2
  15.2 5.1 %mlp.1 = bf16[2048,256]{1,0:T(8,128)(2,1)} custom-call(bf16[2048,256]{1,0:T(8,128)(2,1)S(1)} %get-tuple-element.8.mid, f32[32,256]{1,0:T(8,128)S(1)} %get-tuple-element.9.coarse, s32[1,2048]{1,0:T(1,128)S(1)} %copy-done.2, f32[1,256]{1,0:T(1,128)S(1)} %get-tuple-element.10.gain_mlp, bf16[256,1024]{1,0:T(8,128)(2,1)S(1)} %copy-done, ...), custom_call_target="tpu_custom_call" | custom-call | tf_op jit(solution)/shard_map/mlp/pallas_call | solution.py:535
Async XLA Ops:
  0.0 15.2 %copy-start = (bf16[256,1024]{1,0:T(8,128)(2,1)S(1)}, bf16[256,1024]{1,0:T(8,128)(2,1)}, u32[]{:S(2)}) copy-start(bf16[256,1024]{1,0:T(8,128)(2,1)} %w_up.1) | copy-start | bytes 1572868
  0.0 15.2 %copy-start.1 = (bf16[1024,256]{1,0:T(8,128)(2,1)S(1)}, bf16[1024,256]{1,0:T(8,128)(2,1)}, u32[]{:S(2)}) copy-start(bf16[1024,256]{1,0:T(8,128)(2,1)} %w_down.1) | copy-start | bytes 1572868
  0.0 15.2 %copy-start.2 = (s32[1,2048]{1,0:T(1,128)S(1)}, s32[1,2048]{1,0:T(1,128)}, u32[]{:S(2)}) copy-start(s32[1,2048]{1,0:T(1,128)} %order.1) | copy-start | bytes 24580

commit v9 on v6

--- a/solution.py
+++ b/solution.py
@@ -300,15 +300,12 @@
         spot = pl.ds(i * chunk, chunk)
         mid[spot, :] = (srt[spot, :].astype(F32) + fine).astype(BF)
 
-    first = direct // 2
     qkv_chunk(0)
     for i in range(chunks):
         if i + 1 < chunks:
             qkv_chunk(i + 1)
         ball_chunk(i)
-        if i == chunks - 2:
-            each(first, 0, relay)
-    each(direct, first, relay)
+    each(direct, 0, relay)
 
     own_tokens = jnp.where(own_block < NO_TOKEN / 2, own_block, 0.0).astype(BF)
     q_c = dot(own_tokens, c_qkv[:, :width])
@@ -421,16 +418,19 @@
         mlp_chunk(i)
     scatter_chunk(chunks - 1)
 
+    share = chunk // 2
+    shares = rows // share
+
     def leave(i):
-        spot = pl.ds(i * chunk, chunk)
+        spot = pl.ds(i * share, share)
         return pltpu.make_async_copy(packed.at[spot, :], out.at[spot, :], out_sem.at[i])
 
-    for i in range(chunks):
-        packed[pl.ds(i * chunk, chunk), :] = jnp.concatenate(
-            [ready[pl.ds(2 * i * chunk + n, chunk, stride=2), :] for n in range(width // LANES)], axis=1
+    for i in range(shares):
+        packed[pl.ds(i * share, share), :] = jnp.concatenate(
+            [ready[pl.ds(2 * i * share + n, share, stride=2), :] for n in range(width // LANES)], axis=1
         ).astype(BF)
         leave(i).start()
-    for i in range(chunks):
+    for i in range(shares):
         leave(i).wait()
 
 
@@ -529,7 +529,7 @@
             pltpu.VMEM((1, rows), jnp.int32),
             pltpu.SMEM((1, rows), jnp.int32),
             dma,
-            dma((chunks,)),
+            dma((2 * chunks,)),
         ],
         compiler_params=pltpu.CompilerParams(vmem_limit_bytes=VMEM_MLP),
         name="mlp",

time: 19.4 us -> 19.4 us (level)
  no operation moved by 1% of the time
where the time goes in v9:
time: 19.4 us; the launch traced here: 19.2 us
  Pallas kernels  19.2 us (99%)
    pallas_call x1, Pallas kernels, on_device(): pl.pallas_call(functools.partial(attend_kernel, (*sizes, heads)), out_sha...  14.1 us
    pallas_call x1, Pallas kernels, on_device(): pl.pallas_call(mlp_kernel, out_shape=jax.ShapeDtypeStruct(points.shape, p...  5.1 us

profile of v9, /device:TPU:0, one launch (start us, length us, event | category | flops | bytes accessed | tf_op | source)
XLA Modules:
  0.0 19.2 jit_solution(16315044650213362653)
XLA Ops:
  0.0 0.0 copy-start
  0.0 0.0 copy-start.1
  0.0 0.0 copy-start.2
  0.0 14.1 %attend.1 = (bf16[2048,256]{1,0:T(8,128)(2,1)S(1)}, f32[32,256]{1,0:T(8,128)S(1)}, f32[1,256]{1,0:T(1,128)S(1)}) custom-call(bf16[2048,256]{1,0:T(8,128)(2,1)} %points_hbm.1, s32[1,2048]{1,0:T(1,128)} %order.1, s32[16]{0:T(128)} %counts_hbm.1, f32[1,256]{1,0:T(1,128)} %bitcast.2, f32[2,8]{1,0:T(2,128)} %temps_hbm.1, bf16[256,768]{1,0:T(8,128)(2,1)} %w_qkv_hbm.1, ...), custom_call_target="tpu_custom_call" | custom-call | tf_op jit(solution)/shard_map/attend/pallas_call | solution.py:463
  14.1 0.0 copy-done
  14.1 0.0 copy-done.1
  14.1 0.0 copy-done.2
  14.1 5.1 %mlp.1 = bf16[2048,256]{1,0:T(8,128)(2,1)} custom-call(bf16[2048,256]{1,0:T(8,128)(2,1)S(1)} %get-tuple-element.8.mid, f32[32,256]{1,0:T(8,128)S(1)} %get-tuple-element.9.coarse, s32[1,2048]{1,0:T(1,128)S(1)} %copy-done.2, f32[1,256]{1,0:T(1,128)S(1)} %get-tuple-element.10.gain_mlp, bf16[256,1024]{1,0:T(8,128)(2,1)S(1)} %copy-done, ...), custom_call_target="tpu_custom_call" | custom-call | tf_op jit(solution)/shard_map/mlp/pallas_call | solution.py:520
Async XLA Ops:
  0.0 14.1 %copy-start = (bf16[256,1024]{1,0:T(8,128)(2,1)S(1)}, bf16[256,1024]{1,0:T(8,128)(2,1)}, u32[]{:S(2)}) copy-start(bf16[256,1024]{1,0:T(8,128)(2,1)} %w_up.1) | copy-start | bytes 1572868
  0.0 14.1 %copy-start.1 = (bf16[1024,256]{1,0:T(8,128)(2,1)S(1)}, bf16[1024,256]{1,0:T(8,128)(2,1)}, u32[]{:S(2)}) copy-start(bf16[1024,256]{1,0:T(8,128)(2,1)} %w_down.1) | copy-start | bytes 1572868
  0.0 14.1 %copy-start.2 = (s32[1,2048]{1,0:T(1,128)S(1)}, s32[1,2048]{1,0:T(1,128)}, u32[]{:S(2)}) copy-start(s32[1,2048]{1,0:T(1,128)} %order.1) | copy-start | bytes 24580
